TPU v7x, 32 devices: a whole 2x2x4 slice. The times are simulated.
32 devices in a mesh: row: 8 (over z, x), col: 4 (over y, core).
Axes of the slice: x: 2, y: 2, z: 4, core: 2. Of those that a mesh axis runs over, the one named last changes fastest.
Arguments:
- geneo_vectors: bfloat16 [32, 32, 512, 512], P(None, None, 'row', 'col'), as said below
- phase_labels: int32 [32, 512, 512], P(None, 'row', 'col'), may hold values from 0 to 3, as said below
- phase_mobility: float32 [4], replicated, may hold values from 0.5 to 5
Outputs:
- coarse_factor: float32 [32, 4, 4, 2, 2, 8, 2, 32], P(None, None, 'col', None, None, 'row')
Inputs may be any that keep to these rules, and one draw needn't show every extreme that they name: `geneo_vectors`: the 32 vectors of each subdomain are linearly independent on its cells. `phase_labels`: within one subdomain the labels take one or two values, some q and (q + 1) modulo 4.
All inputs are finite; a program needn't handle non-finite values.
Results may differ from a plain program's by a relative error of at most 0.00055.
Values may be sent and summed in bfloat16 or wider, within the bound.
A program may use at most 512 MiB of HBM per device.

v0:
```python
import jax
import jax.numpy as jnp
from jax import lax
from jax.experimental import pallas as pl
from jax.experimental.pallas import tpu as pltpu
from jax.sharding import PartitionSpec as P

NB = 2
PSUB = 2


FACES = ((-1, 0), (1, 0), (0, -1), (0, 1))


def with_halo(cells, sides, width):
    for axis, dim in sides:
        count = lax.axis_size(axis)
        ends = count - 1
        head = lax.slice_in_dim(cells, 0, width, axis=dim)
        tail = lax.slice_in_dim(cells, cells.shape[dim] - width, cells.shape[dim], axis=dim)
        cells = jnp.concatenate(
            [
                lax.ppermute(tail, axis, [(i, (i + 1) % count) for i in range(ends)]),
                cells,
                lax.ppermute(head, axis, [((i + 1) % count, i) for i in range(ends)]),
            ],
            axis=dim,
        )
    return cells


def slot_offsets():
    offsets = [((0, 0), (0, 0))]
    for face in FACES:
        offsets += [((0, 0), face), (face, (0, 0)), (face, face)]
    for face_x in FACES[:2]:
        for face_y in FACES[2:]:
            offsets += [(face_x, face_y), (face_y, face_x)]
    return offsets


def band_index(from_off, to_off):
    return (to_off[0] - from_off[0] + 1) * 3 + (to_off[1] - from_off[1] + 1)


def from_next(field, axis):
    count = field.shape[axis]
    inner = lax.slice_in_dim(field, 1, count, axis=axis)
    blank = jnp.zeros_like(lax.slice_in_dim(field, 0, 1, axis=axis))
    return jnp.concatenate([inner, blank], axis=axis)


def from_prev(field, axis):
    count = field.shape[axis]
    inner = lax.slice_in_dim(field, 0, count - 1, axis=axis)
    blank = jnp.zeros_like(lax.slice_in_dim(field, 0, 1, axis=axis))
    return jnp.concatenate([blank, inner], axis=axis)


def laplace_own(own):
    field = own.astype(jnp.float32)
    near = from_next(field, 1) + from_prev(field, 1)
    near = near + from_next(field, 2) + from_prev(field, 2)
    near = near + from_next(field, 3) + from_prev(field, 3)
    return near - 6.0 * field


def contract_cells(left, right):
    flat_left = left.reshape(left.shape[0], -1)
    flat_right = right.reshape(right.shape[0], -1)
    return lax.dot_general(
        flat_left, flat_right, (((1,), (1,)), ((), ())), preferred_element_type=jnp.float32
    )


SUBL = 16


def flux_gram_kernel(prev_ref, cur_ref, next_ref, root_ref, acc_ref, fx_ref, edge_ref, flux_ref):
    z = pl.program_id(0)
    n_z = pl.num_programs(0)
    vectors, n_x, n_y = flux_ref.shape
    half = n_y // 2

    @pl.when(z == 0)
    def _():
        acc_ref[...] = jnp.zeros_like(acc_ref)
        edge_ref[...] = jnp.zeros_like(edge_ref)

    use_prev = (z > 0).astype(jnp.float32)
    use_next = (z < n_z - 1).astype(jnp.float32)

    def step(v, carry):
        rows = lax.broadcasted_iota(jnp.int32, (n_x, n_y), 0)
        lanes = lax.broadcasted_iota(jnp.int32, (n_x, n_y), 1)
        own = cur_ref[v, 0].astype(jnp.float32)
        near = next_ref[v, 0].astype(jnp.float32) * use_next
        near = near + prev_ref[v, 0].astype(jnp.float32) * use_prev
        near = near + jnp.where(rows == n_x - 1, 0.0, pltpu.roll(own, n_x - 1, 0))
        near = near + jnp.where(rows == 0, 0.0, pltpu.roll(own, 1, 0))
        near = near + jnp.where(lanes == n_y - 1, 0.0, pltpu.roll(own, n_y - 1, 1))
        near = near + jnp.where(lanes == 0, 0.0, pltpu.roll(own, 1, 1))
        flux = ((near - 6.0 * own) * root_ref[0]).astype(jnp.bfloat16)
        flux_ref[v] = flux
        wide = flux.astype(jnp.float32)
        fx_ref[v, 0, 0:1, :] = wide[0:1, :]
        fx_ref[v, 0, 1:2, :] = wide[n_x - 1 : n_x, :]
        turned_f = pltpu.roll(wide, 2 * z + 1, 1)
        turned_o = pltpu.roll(own, 2 * z + 1 + half, 1)
        kept = edge_ref[v]
        is_f = (lanes >= 2 * z) & (lanes < 2 * z + 2)
        is_o = (lanes >= 2 * z + half) & (lanes < 2 * z + 2 + half)
        edge_ref[v] = jnp.where(is_f, turned_f, jnp.where(is_o, turned_o, kept))
        return carry

    lax.fori_loop(0, vectors, step, 0)
    for block in range(n_x // SUBL):
        span = slice(block * SUBL, (block + 1) * SUBL)
        left = cur_ref[:, 0, span, :].reshape(vectors * SUBL, n_y)
        right = flux_ref[:, span, :].reshape(vectors * SUBL, n_y)
        both = jnp.concatenate([left, right], axis=1)
        acc_ref[...] += lax.dot_general(
            both, both, (((1,), (1,)), ((), ())), preferred_element_type=jnp.float32
        )


def flux_gram(own, cell_root):
    vectors, n_z, n_x, n_y = own.shape
    order = vectors * SUBL
    block = (vectors, 1, n_x, n_y)
    acc, flux_x, edges = pl.pallas_call(
        flux_gram_kernel,
        grid=(n_z,),
        in_specs=[
            pl.BlockSpec(block, lambda z: (0, jnp.maximum(z - 1, 0), 0, 0)),
            pl.BlockSpec(block, lambda z: (0, z, 0, 0)),
            pl.BlockSpec(block, lambda z: (0, jnp.minimum(z + 1, n_z - 1), 0, 0)),
            pl.BlockSpec((1, n_x, n_y), lambda z: (z, 0, 0)),
        ],
        out_specs=[
            pl.BlockSpec((order, order), lambda z: (0, 0)),
            pl.BlockSpec((vectors, 1, 2, n_y), lambda z: (0, z, 0, 0)),
            pl.BlockSpec((vectors, n_x, n_y), lambda z: (0, 0, 0)),
        ],
        out_shape=[
            jax.ShapeDtypeStruct((order, order), jnp.float32),
            jax.ShapeDtypeStruct((vectors, n_z, 2, n_y), jnp.float32),
            jax.ShapeDtypeStruct((vectors, n_x, n_y), jnp.float32),
        ],
        scratch_shapes=[pltpu.VMEM((vectors, n_x, n_y), jnp.bfloat16)],
        compiler_params=pltpu.CompilerParams(vmem_limit_bytes=40 * 1024 * 1024),
    )(own, own, own, cell_root)
    place = jnp.arange(order, dtype=jnp.int32) % SUBL
    acc = jnp.where(place[:, None] == place[None, :], acc, jnp.float32(0.0))
    half_sum = acc.reshape(vectors, SUBL, order).sum(1)
    gram = half_sum.reshape(vectors, vectors, SUBL).sum(2)
    half = n_y // 2
    edges = edges.astype(jnp.bfloat16)
    flux_edge = edges[:, :, : 2 * n_z].reshape(vectors, n_x, n_z, 2)
    own_edge = edges[:, :, half : half + 2 * n_z].reshape(vectors, n_x, n_z, 2)
    return gram, flux_x.astype(jnp.bfloat16), flux_edge, own_edge


def local_tiles(own, labels, mobility_table):
    rims_x = jnp.stack([own[:, :, 0, :], own[:, :, -1, :]], axis=2)
    wide_x = with_halo(rims_x, (("row", 2),), 1)
    lower_x = wide_x[:, :, 0, :]
    upper_x = wide_x[:, :, 3, :]
    root_table = jnp.sqrt(mobility_table)
    cell_root = jnp.zeros(labels.shape, jnp.float32)
    for phase in range(mobility_table.shape[0]):
        cell_root = cell_root + jnp.where(labels == phase, root_table[phase], jnp.float32(0.0))
    gram, flux_x, flux_edge, own_edge = flux_gram(own, cell_root)
    tiles = [gram]
    count = lax.axis_size("col")
    lower_y = lax.ppermute(own_edge[..., 0], "col", [(i, i + 1) for i in range(count - 1)])
    upper_y = lax.ppermute(own_edge[..., 1], "col", [(i + 1, i) for i in range(count - 1)])
    face_data = [
        (flux_x[:, :, 0, :], lower_x, cell_root[:, 0, :]),
        (flux_x[:, :, 1, :], upper_x, cell_root[:, -1, :]),
        (flux_edge[..., 1], lower_y, cell_root[:, :, 0].T),
        (flux_edge[..., 0], upper_y, cell_root[:, :, -1].T),
    ]
    for layer_f, layer_z, layer_r in face_data:
        across = (layer_z.astype(jnp.float32) * layer_r).astype(jnp.bfloat16)
        cross = contract_cells(layer_f, across)
        tiles += [cross, cross.T, contract_cells(across, across)]
    for x_first in (True, False):
        for y_first in (True, False):
            layer_x = lower_x if x_first else upper_x
            layer_y = lower_y if y_first else upper_y
            cell_x = 0 if x_first else -1
            cell_y = 0 if y_first else -1
            corner_r = cell_root[:, cell_x, cell_y]
            along_x = (layer_x[:, :, cell_y].astype(jnp.float32) * corner_r).astype(jnp.bfloat16)
            along_y = (layer_y[:, cell_x, :].astype(jnp.float32) * corner_r).astype(jnp.bfloat16)
            pair = contract_cells(along_x, along_y)
            tiles += [pair, pair.T]
    return jnp.stack(tiles)


def shift_grid(values, offset):
    widths = [(1, 1), (1, 1)] + [(0, 0)] * (values.ndim - 2)
    padded = jnp.pad(values, widths)
    start_x = 1 - offset[0]
    start_y = 1 - offset[1]
    return padded[start_x : start_x + values.shape[0], start_y : start_y + values.shape[1]]


def to_owner(stack, n_row, n_col):
    slots = stack.shape[0]
    vectors = stack.shape[1]
    row_blocks = vectors // (NB * n_row)
    col_blocks = vectors // (NB * n_col)
    split = stack.reshape(slots, row_blocks, n_row, NB, col_blocks, n_col, NB)
    moved = split.transpose(2, 5, 0, 4, 6, 1, 3)
    return moved.reshape(n_row, n_col, slots * col_blocks * NB * row_blocks * NB)


def place_bands(bands, n_row, n_col):
    n_sub = n_row * n_col
    sub_x = jnp.arange(n_sub, dtype=jnp.int32) // n_col
    sub_y = jnp.arange(n_sub, dtype=jnp.int32) % n_col
    total = None
    for index in range(9):
        step_x = index // 3 - 1
        step_y = index % 3 - 1
        match = (
            (sub_x[:, None] == sub_x[None, :] + step_x)
            & (sub_y[:, None] == sub_y[None, :] + step_y)
        ).astype(jnp.float32)
        flat = bands[index].reshape(n_sub, -1).T
        term = match[:, None, :] * flat[None, :, :]
        total = term if total is None else total + term
    return total


def body(geneo_vectors, phase_labels, phase_mobility):
    vectors = geneo_vectors.shape[0]
    n_row = lax.axis_size("row")
    n_col = lax.axis_size("col")
    n_sub = n_row * n_col
    row_blocks = vectors // (NB * n_row)
    col_blocks = vectors // (NB * n_col)
    rows_here = row_blocks * NB * n_sub
    piece_len = col_blocks * NB * row_blocks * NB
    width = PSUB * vectors
    tiles = local_tiles(geneo_vectors, phase_labels, phase_mobility)
    offsets = slot_offsets()
    routed = lax.all_to_all(
        lax.all_to_all(
            to_owner(tiles, n_row, n_col), "row", split_axis=0, concat_axis=0, tiled=True
        ),
        "col",
        split_axis=1,
        concat_axis=1,
        tiled=True,
    )
    routed = routed.reshape(n_row, n_col, len(offsets), piece_len)
    bands = [jnp.zeros((n_row, n_col, piece_len), jnp.float32) for count in range(9)]
    for slot, pair_off in enumerate(offsets):
        place = band_index(pair_off[0], pair_off[1])
        bands[place] = bands[place] + shift_grid(routed[:, :, slot], pair_off[0])
    local = place_bands(bands, n_row, n_col).reshape(n_sub, col_blocks * NB, rows_here)
    row_index = lax.axis_index("row")
    col_index = lax.axis_index("col")
    row_sub = jnp.arange(rows_here, dtype=jnp.int32) % n_sub
    ends = 2 * PSUB
    mine = local[:ends].reshape(ends, col_blocks, NB, rows_here)
    parts = lax.all_gather(mine, ("row", "col"), axis=0, tiled=False)
    parts = parts.reshape(n_row, n_col, ends, col_blocks, NB, rows_here)
    panels = parts.transpose(2, 3, 1, 4, 0, 5).reshape(2, width, n_row, rows_here)

    def rows_of(block, first, last):
        grid = block.reshape(width, n_row, row_blocks, NB, n_sub)[..., first:last]
        return grid.transpose(0, 4, 2, 1, 3).reshape(width, (last - first) * vectors)

    done = []
    for panel in range(2):
        first = panel * PSUB
        last = first + PSUB
        block = panels[panel]
        for solved in done:
            change = lax.dot_general(
                rows_of(solved, first, last),
                solved.reshape(width, n_row * rows_here),
                (((0,), (0,)), ((), ())),
                precision=lax.Precision.HIGHEST,
                preferred_element_type=jnp.float32,
            )
            block = block - change.reshape(width, n_row, rows_here)
        block = jnp.where(row_sub >= first, block, jnp.float32(0.0))
        low = jnp.linalg.cholesky(rows_of(block, first, last).T)
        solved = lax.linalg.triangular_solve(
            low, block.reshape(width, n_row * rows_here), left_side=True, lower=True
        ).reshape(width, n_row, rows_here)
        done.append(solved)
    both = jnp.concatenate(done, axis=0)
    rows_mine = lax.dynamic_index_in_dim(both, row_index, 1, keepdims=False)
    by_block = both.reshape(2 * width, n_row, row_blocks, NB, n_sub).transpose(0, 2, 1, 3, 4)
    picked = lax.dynamic_index_in_dim(
        by_block.reshape(2 * width, row_blocks, n_row // n_col, n_col, NB, n_sub),
        col_index,
        3,
        keepdims=False,
    )
    columns = (
        picked.reshape(2 * width, col_blocks * NB, n_sub)
        .transpose(0, 2, 1)
        .reshape(2 * width, n_sub * col_blocks * NB)
    )
    update = lax.dot_general(
        columns,
        rows_mine,
        (((0,), (0,)), ((), ())),
        precision=lax.Precision.HIGHEST,
        preferred_element_type=jnp.float32,
    ).reshape(n_sub, col_blocks * NB, rows_here)
    panel_mine = lax.dynamic_index_in_dim(
        rows_mine.reshape(ends, col_blocks, n_col, NB, rows_here), col_index, 2, keepdims=False
    ).reshape(ends, col_blocks * NB, rows_here)
    rest = jnp.where(row_sub < ends, jnp.float32(0.0), local[ends:] - update[ends:])
    local = jnp.concatenate([panel_mine, rest], axis=0)
    return local.reshape(n_sub, col_blocks, 1, NB, row_blocks, 1, NB, n_sub)


def solution(mesh):
    return jax.shard_map(
        body,
        mesh=mesh,
        in_specs=(P(None, None, "row", "col"), P(None, "row", "col"), P()),
        out_specs=P(None, None, "col", None, None, "row", None, None),
        check_vma=False,
    )
```

profile of v0, /device:TPU:0, one launch (start us, length us, event | category | flops | bytes accessed | tf_op | source)
XLA Modules:
  0.0 454.9 jit_solution(1287684262653949693)
XLA Ops:
  0.0 3.3 fusion.81
  4.1 4.9 %collective-permute-start = (bf16[32,32,1,128]{3,1,0,2:T(8,128)(2,1)}, bf16[32,32,1,128]{3,1,0,2:T(8,128)(2,1)S(1)}, u32[]{:S(2)}, u32[]{:S(2)}) collective-permute-start(bf16[32,32,1,128]{3,1,0,2:T(8,128)(2,1)} %copy.489), channel_id=1, source_target_pairs={{0,4},{4,8},{8,12},{12,16},{16,20},{20,24},{24,28},{1,5},{5,9},{9,... | collective-permute-start | bytes 786440 | tf_op jit(solution)/shard_map/ppermute | solution.py:23
  9.7 1.3 collective-permute-start.1
  12.4 4.2 select_add_fusion.root_ref
  16.5 185.3 %shard_map.37 = (f32[512,512]{1,0:T(8,128)S(1)}, f32[32,32,2,128]{3,2,1,0:T(2,128)S(1)}, f32[32,64,128]{2,1,0:T(8,128)S(1)}) custom-call(bf16[32,32,64,128]{3,2,1,0:T(8,128)(2,1)} %next_ref.1, bf16[32,32,64,128]{3,2,1,0:T(8,128)(2,1)} %next_ref.1, bf16[32,32,64,128]{3,2,1,0:T(8,128)(2,1)} %next_ref.1, f32[32,64,128]{2,1,0:T(8,128)S(1)} %select_add_fusion.root_ref), custom_call_target="tpu_custom_call" | custom-call | tf_op jit(solution)/shard_map/pallas_call | solution.py:131
  201.9 1.2 fusion.86
  203.1 2.5 copy.351
  205.6 1.9 fusion.84
  207.5 2.6 copy.491
  210.1 2.3 collective-permute-start.2
  212.4 2.6 copy.492
  215.0 1.7 collective-permute-start.3
  221.3 3.4 copy.371
  225.1 2.1 fusion.87
  227.2 1.8 copy.349
  231.1 1.5 fusion.48
  232.6 1.5 slice_reduce_fusion.2
  234.1 1.2 multiply_convert_fusion.1
  236.5 3.1 copy.378
  239.8 3.4 copy.379
  243.2 1.2 multiply_convert_fusion
  244.6 1.2 reshape.852
  245.8 1.1 fusion.92
  247.3 3.5 copy.380
  250.8 1.1 reshape.896
  251.9 4.0 copy.381
  256.8 5.1 %copy.382 = f32[1,2,8,2,4,4,2]{0,2,6,5,4,3,1:T(8,128)} copy(f32[1,2,8,2,4,4,2]{3,2,1,6,5,4,0:T(8,128)} %stack.71) | data formatting | bytes 8192 | tf_op jit(solution)/shard_map/stack | solution.py:199
  263.1 5.1 %copy.383 = f32[1,2,8,2,4,4,2]{0,2,6,5,4,3,1:T(8,128)} copy(f32[1,2,8,2,4,4,2]{3,2,1,6,5,4,0:T(8,128)} %stack.72) | data formatting | bytes 8192 | tf_op jit(solution)/shard_map/stack | solution.py:199
  269.0 1.5 fusion.20
  270.5 1.5 multiply_convert_fusion.7
  272.0 1.1 reshape.893
  273.1 4.8 %copy.372 = f32[1,2,8,2,4,4,2]{0,2,6,5,4,3,1:T(8,128)} copy(f32[1,2,8,2,4,4,2]{6,5,4,3,2,1,0:T(4,128)} %reshape.893) | data formatting | bytes 8192 | tf_op jit(solution)/shard_map/stack | solution.py:199
  278.8 5.1 %copy.373 = f32[1,2,8,2,4,4,2]{0,2,6,5,4,3,1:T(8,128)} copy(f32[1,2,8,2,4,4,2]{3,2,1,6,5,4,0:T(8,128)} %stack.64) | data formatting | bytes 8192 | tf_op jit(solution)/shard_map/stack | solution.py:199
  283.9 1.9 convolution_bitcast_fusion.1
  285.8 1.6 copy.374
  287.4 1.0 fusion.106
  288.5 1.5 fusion.15
  290.0 1.1 reshape.894
  291.1 4.8 %copy.375 = f32[1,2,8,2,4,4,2]{0,2,6,5,4,3,1:T(8,128)} copy(f32[1,2,8,2,4,4,2]{6,5,4,3,2,1,0:T(4,128)} %reshape.894) | data formatting | bytes 8192 | tf_op jit(solution)/shard_map/stack | solution.py:199
  296.8 5.1 %copy.376 = f32[1,2,8,2,4,4,2]{0,2,6,5,4,3,1:T(8,128)} copy(f32[1,2,8,2,4,4,2]{3,2,1,6,5,4,0:T(8,128)} %stack.66) | data formatting | bytes 8192 | tf_op jit(solution)/shard_map/stack | solution.py:199
  301.9 1.0 multiply_convert_fusion.6
  303.8 1.6 copy.377
  305.4 2.7 fusion.4
  309.3 3.9 copy.384
  313.4 4.2 copy.385
  318.7 3.9 copy.386
  322.8 4.2 copy.387
  328.1 3.9 copy.388
  332.2 4.2 copy.389
  337.6 3.9 copy.390
  341.7 4.1 copy.391
  345.8 8.0 %stack.81 = f32[21,2,8,2,4,4,2]{0,2,6,5,4,3,1:T(8,128)} concatenate(f32[1,2,8,2,4,4,2]{0,2,6,5,4,3,1:T(8,128)S(1)} %copy.371, f32[1,2,8,2,4,4,2]{0,2,6,5,4,3,1:T(8,128)} %copy.372, f32[1,2,8,2,4,4,2]{0,2,6,5,4,3,1:T(8,128)} %copy.373, f32[1,2,8,2,4,4,2]{0,2,6,5,4,3,1:T(8,128)} %copy.374, f32[1,2,8,2,4,4,2]{0,2,6,5,4,3,1:T(8,128)} %copy.375, f32[1,2,8,2,4,4,2]{0,2,6,5,4,3,1:T(8,128)} %copy.376, ...), dimensions={0} | concatenate | bytes 172032 | tf_op jit(solution)/shard_map/stack | solution.py:199
  353.8 2.9 copy.392
  356.7 1.1 copy.393
  357.8 7.5 %all-to-all-start = ((f32[8,4,672]{2,1,0:T(4,128)}), f32[8,4,672]{2,1,0:T(4,128)S(1)}, u32[]{:S(2)}, u32[]{:S(2)}) async-start(f32[8,4,672]{2,1,0:T(4,128)} %copy.393), calls=%async_computation | async-start | bytes 196608 | tf_op jit(solution)/shard_map/all_to_all | solution.py:251
  365.9 6.5 %all-to-all-done = f32[8,4,672]{2,1,0:T(4,128)S(1)} async-done(((f32[8,4,672]{2,1,0:T(4,128)}), f32[8,4,672]{2,1,0:T(4,128)S(1)}, u32[]{:S(2)}, u32[]{:S(2)}) %all-to-all-start) | async-done | bytes 86048 | tf_op jit(solution)/shard_map/all_to_all | solution.py:251
  373.0 5.0 %all-to-all-start.1 = ((f32[8,4,672]{2,0,1:T(8,128)}), f32[8,4,672]{2,0,1:T(8,128)S(1)}, u32[]{:S(2)}, u32[]{:S(2)}) async-start(f32[8,4,672]{2,0,1:T(8,128)} %copy.394), calls=%async_computation.1 | async-start | bytes 196608 | tf_op jit(solution)/shard_map/all_to_all | solution.py:250
  378.0 4.3 all-to-all-done.1
  384.2 38.5 %all_gather.3 = f32[32,4,4,2,128]{4,2,3,1,0:T(4,128)S(1)} all-gather(f32[1,4,4,2,128]{4,2,3,1,0:T(4,128)S(1)} %copy.425), channel_id=1, replica_groups=mesh['row'=8,'col'=4] {'row','col'}, dimensions={0}, use_global_device_ids=true | all-gather | bytes 540672 | tf_op jit(solution)/shard_map/all_gather | solution.py:270
  425.4 5.8 %cholesky.44 = f32[64,64]{1,0:T(8,128)S(1)} custom-call(f32[64,64]{1,0:T(8,128)S(1)} %add_multiply_fusion.1), custom_call_target="Cholesky" | custom-call | tf_op jit(solution)/shard_map/jit(cholesky)/cholesky | solution.py:293
  432.6 4.9 %custom-call.6 = f32[1,64,64]{1,2,0:T(8,128)S(1)} custom-call(f32[1,64,64]{2,1,0:T(8,128)S(1)} %fusion.32), custom_call_target="InvertDiagBlocksLowerTriangular" | custom-call | tf_op jit(solution)/shard_map/triangular_solve/custom-call.0 | solution.py:294
  439.2 5.8 %cholesky.55 = f32[64,64]{1,0:T(8,128)S(1)} custom-call(f32[64,64]{1,0:T(8,128)S(1)} %add_multiply_fusion), custom_call_target="Cholesky" | custom-call | tf_op jit(solution)/shard_map/jit(cholesky)/cholesky | solution.py:293
  446.4 4.9 %custom-call.7 = f32[1,64,64]{1,2,0:T(8,128)S(1)} custom-call(f32[1,64,64]{2,1,0:T(8,128)S(1)} %fusion.33), custom_call_target="InvertDiagBlocksLowerTriangular" | custom-call | tf_op jit(solution)/shard_map/triangular_solve/custom-call.0 | solution.py:294
  453.4 1.1 pad_maximum_fusion.1
  (155 shorter events, 34.7 us)
Async XLA Ops:
  4.1 264.1 %collective-permute-start = (bf16[32,32,1,128]{3,1,0,2:T(8,128)(2,1)}, bf16[32,32,1,128]{3,1,0,2:T(8,128)(2,1)S(1)}, u32[]{:S(2)}, u32[]{:S(2)}) collective-permute-start(bf16[32,32,1,128]{3,1,0,2:T(8,128)(2,1)} %copy.489), channel_id=1, source_target_pairs={{0,4},{4,8},{8,12},{12,16},{16,20},{20,24},{24,28},{1,5},{5,9},{9,... | collective-permute-start | bytes 786440 | tf_op jit(solution)/shard_map/ppermute | solution.py:23
  9.7 277.7 %collective-permute-start.1 = (bf16[32,32,1,128]{3,1,0,2:T(8,128)(2,1)}, bf16[32,32,1,128]{3,1,0,2:T(8,128)(2,1)}, u32[]{:S(2)}, u32[]{:S(2)}) collective-permute-start(bf16[32,32,1,128]{3,1,0,2:T(8,128)(2,1)} %copy.490), channel_id=1, source_target_pairs={{4,0},{8,4},{12,8},{16,12},{20,16},{24,20},{28,24},{5,1},{9,5},{13... | collective-permute-start | bytes 786440 | tf_op jit(solution)/shard_map/ppermute | solution.py:25
  210.1 24.0 %collective-permute-start.2 = (bf16[32,64,32]{2,0,1:T(8,128)(2,1)}, bf16[32,64,32]{2,0,1:T(8,128)(2,1)}, u32[]{:S(2)}, u32[]{:S(2)}) collective-permute-start(bf16[32,64,32]{2,0,1:T(8,128)(2,1)} %bitcast.301), channel_id=1, source_target_pairs={{0,1},{1,2},{2,3},{4,5},{5,6},{6,7},{8,9},{9,10},{10,11},{12,13},{... | collective-permute-start | bytes 393224 | tf_op jit(solution)/shard_map/ppermute | solution.py:176
  215.0 28.2 %collective-permute-start.3 = (bf16[32,64,32]{2,0,1:T(8,128)(2,1)}, bf16[32,64,32]{2,0,1:T(8,128)(2,1)}, u32[]{:S(2)}, u32[]{:S(2)}) collective-permute-start(bf16[32,64,32]{2,0,1:T(8,128)(2,1)} %bitcast.300), channel_id=1, source_target_pairs={{1,0},{2,1},{3,2},{5,4},{6,5},{7,6},{9,8},{10,9},{11,10},{13,12},{... | collective-permute-start | bytes 393224 | tf_op jit(solution)/shard_map/ppermute | solution.py:177
  262.2 83.6 %copy-start = (f32[1,2,8,2,4,4,2]{0,2,6,5,4,3,1:T(8,128)S(1)}, f32[1,2,8,2,4,4,2]{0,2,6,5,4,3,1:T(8,128)}, u32[]{:S(2)}) copy-start(f32[1,2,8,2,4,4,2]{0,2,6,5,4,3,1:T(8,128)} %copy.382) | copy-start | bytes 12292
  288.4 95.2 %copy-start.1 = (f32[32,32]{1,0:T(8,128)S(1)}, f32[32,32]{1,0:T(8,128)}, u32[]{:S(2)}) copy-start(f32[32,32]{1,0:T(8,128)} %get-tuple-element.58) | copy-start | bytes 12292
  288.5 95.2 %copy-start.2 = (f32[32,32]{1,0:T(8,128)S(1)}, f32[32,32]{1,0:T(8,128)}, u32[]{:S(2)}) copy-start(f32[32,32]{1,0:T(8,128)} %get-tuple-element.59) | copy-start | bytes 12292
  288.5 95.2 %copy-start.3 = (f32[32,32]{1,0:T(8,128)S(1)}, f32[32,32]{1,0:T(8,128)}, u32[]{:S(2)}) copy-start(f32[32,32]{1,0:T(8,128)} %get-tuple-element.60) | copy-start | bytes 12292
  288.5 95.2 %copy-start.4 = (f32[32,32]{1,0:T(8,128)S(1)}, f32[32,32]{1,0:T(8,128)}, u32[]{:S(2)}) copy-start(f32[32,32]{1,0:T(8,128)} %get-tuple-element.61) | copy-start | bytes 12292
  288.5 95.2 %copy-start.5 = (f32[32,32]{1,0:T(8,128)S(1)}, f32[32,32]{1,0:T(8,128)}, u32[]{:S(2)}) copy-start(f32[32,32]{1,0:T(8,128)} %get-tuple-element.62) | copy-start | bytes 12292
  305.4 78.3 %copy-start.6 = (f32[32,32]{1,0:T(8,128)S(1)}, f32[32,32]{1,0:T(8,128)}, u32[]{:S(2)}) copy-start(f32[32,32]{1,0:T(8,128)} %get-tuple-element.63) | copy-start | bytes 12292
  305.4 78.3 %copy-start.7 = (f32[32,32]{1,0:T(8,128)S(1)}, f32[32,32]{1,0:T(8,128)}, u32[]{:S(2)}) copy-start(f32[32,32]{1,0:T(8,128)} %get-tuple-element.64) | copy-start | bytes 12292
  305.4 78.3 %copy-start.8 = (f32[32,32]{1,0:T(8,128)S(1)}, f32[32,32]{1,0:T(8,128)}, u32[]{:S(2)}) copy-start(f32[32,32]{1,0:T(8,128)} %get-tuple-element.65) | copy-start | bytes 12292
  341.6 42.1 %copy-start.9 = (f32[32,32]{1,0:T(8,128)S(1)}, f32[32,32]{1,0:T(8,128)}, u32[]{:S(2)}) copy-start(f32[32,32]{1,0:T(8,128)} %get-tuple-element.66) | copy-start | bytes 12292
  345.8 92.7 %copy-start.10 = (pred[128]{0:T(512)(128)(4,1)S(1)}, pred[128]{0:T(512)(128)(4,1)}, u32[]{:S(2)}) copy-start(pred[128]{0:T(512)(128)(4,1)} %get-tuple-element.75) | copy-start | bytes 388
  357.8 14.6 %all-to-all-start = ((f32[8,4,672]{2,1,0:T(4,128)}), f32[8,4,672]{2,1,0:T(4,128)S(1)}, u32[]{:S(2)}, u32[]{:S(2)}) async-start(f32[8,4,672]{2,1,0:T(4,128)} %copy.393), calls=%async_computation | async-start | bytes 196608 | tf_op jit(solution)/shard_map/all_to_all | solution.py:251
  373.0 9.3 %all-to-all-start.1 = ((f32[8,4,672]{2,0,1:T(8,128)}), f32[8,4,672]{2,0,1:T(8,128)S(1)}, u32[]{:S(2)}, u32[]{:S(2)}) async-start(f32[8,4,672]{2,0,1:T(8,128)} %copy.394), calls=%async_computation.1 | async-start | bytes 196608 | tf_op jit(solution)/shard_map/all_to_all | solution.py:250
where the time goes:
time: 460 us; the launch traced here: 455 us
  Pallas kernels  185 us (40%)
  local copies, waits for them, and re-layouts  139 us (30%)
  other arithmetic  44.9 us (10%)
  blocking collectives  38.5 us (8%)
  starting transfers between devices  22.6 us (5%)
  matrix products  12.4 us (3%)
  waiting for transfers between devices  10.8 us (2%)
    pallas_call x1, Pallas kernels, flux_gram(): pl.pallas_call(flux_gram_kernel, grid=(n_z,), in_specs=[pl.BlockSpec(bloc...  185 us
    another operation x39, local copies, waits for them, and re-layouts, local_tiles(): return jnp.stack(tiles)  97.4 us
    all_gather x1, blocking collectives, body(): parts = lax.all_gather(mine, ('row', 'col'), axis=0, tiled=False)  38.5 us
    another operation x6, other arithmetic, body(): low = jnp.linalg.cholesky(rows_of(block, first, last).T)  13 us
    another operation x4, other arithmetic, body(): lax.linalg.triangular_solve(low, block.reshape(width, n_row * rows_here),...  11.1 us
    dot_general x12, matrix products, contract_cells(): lax.dot_general(flat_left, flat_right, (((1,), (1,)), ((), ())), preferre...  10.9 us
  transfers between devices with their start and end apart: 6, of which 2 were waited for; matrix products, arithmetic and copies ran while one was open for 19% of the time, Pallas kernels for 41%

commit v1 on v0

v1 whole, which is shorter than its diff:
```python
import jax
import jax.numpy as jnp
from jax import lax
from jax.experimental import pallas as pl
from jax.experimental.pallas import tpu as pltpu
from jax.sharding import PartitionSpec as P

NB = 2
PSUB = 2


FACES = ((-1, 0), (1, 0), (0, -1), (0, 1))


def slot_offsets():
    offsets = [((0, 0), (0, 0))]
    for face in FACES:
        offsets += [((0, 0), face), (face, (0, 0)), (face, face)]
    for face_x in FACES[:2]:
        for face_y in FACES[2:]:
            offsets += [(face_x, face_y), (face_y, face_x)]
    return offsets


def band_index(from_off, to_off):
    return (to_off[0] - from_off[0] + 1) * 3 + (to_off[1] - from_off[1] + 1)


ROWS = 8
GROUP = 8


def gram_kernel(mob_ref, own_ref, lab_ref, acc_ref, rim_ref, frim_ref, edge_ref, rootx_ref, rooty_ref,
                plain_ref, part_ref, rows_ref, root_ref, lines_ref, side_ref):
    g = pl.program_id(0)
    n_z = pl.num_programs(0) - 1
    vectors, n_x, n_y = edge_ref.shape
    blocks = n_x // ROWS
    groups = vectors // GROUP
    per = blocks // groups
    lanes = lax.broadcasted_iota(jnp.int32, (n_x, n_y), 1)
    now = lax.rem(g, 2)
    old = 1 - now

    @pl.when(g == 0)
    def _():
        acc_ref[...] = jnp.zeros_like(acc_ref)
        side_ref[...] = jnp.zeros_like(side_ref)
        rooty_ref[...] = jnp.zeros_like(rooty_ref)
        plain_ref[...] = jnp.zeros_like(plain_ref)
        part_ref[...] = jnp.zeros_like(part_ref)
        rows_ref[...] = jnp.zeros_like(rows_ref)
        root_ref[...] = jnp.zeros_like(root_ref)

    def gram(slot, j):
        both = rows_ref[slot, j]
        acc_ref[...] += lax.dot_general(both, both, (((1,), (1,)), ((), ())), preferred_element_type=jnp.float32)

    def trip(j, fresh):
        root = root_ref[old]
        spot = pl.multiple_of(j * GROUP * ROWS, GROUP * ROWS)
        line = pl.multiple_of(j * GROUP, GROUP)
        ok = (lanes < 4 * g + 4) & (lanes >= 4 * g)
        fluxes, olds = [], []
        for i in range(GROUP):
            v = j * GROUP + i
            before = plain_ref[old, v, ROWS : ROWS + n_x]
            total = part_ref[v]
            if fresh:
                own = own_ref[v, 0].astype(jnp.float32)
                plain_ref[now, v, ROWS : ROWS + n_x] = own
                total = total + own
                near = plain_ref[now, v, ROWS + 1 : ROWS + 1 + n_x] + plain_ref[now, v, ROWS - 1 : ROWS - 1 + n_x]
                near = near + jnp.where(lanes == n_y - 1, 0.0, pltpu.roll(own, n_y - 1, 1))
                near = near + jnp.where(lanes == 0, 0.0, pltpu.roll(own, 1, 1))
                near = near + before
                part_ref[v] = near - 6.0 * own
                turned = pltpu.roll(own, 4 * g + 2, 1)
                side_ref[v] = jnp.where(ok, turned, side_ref[v])
                lines_ref[0, pl.ds(line + i, 1)] = own[:1]
                lines_ref[1, pl.ds(line + i, 1)] = own[n_x - 1 :]
            flux = total * root
            lines_ref[2, pl.ds(line + i, 1)] = flux[:1]
            lines_ref[3, pl.ds(line + i, 1)] = flux[n_x - 1 :]
            fluxes.append(flux)
            olds.append(before)
            if i % 2:
                for b in range(blocks):
                    part = slice(b * ROWS, b * ROWS + ROWS)
                    where = pl.ds(spot + (i - 1) * ROWS, 2 * ROWS)
                    at = (b % per) * 2 * n_y
                    rows_ref[now, b // per, where, at : at + n_y] = jnp.concatenate(
                        [olds[i - 1][part], olds[i][part]], axis=0).astype(jnp.bfloat16)
                    rows_ref[now, b // per, where, at + n_y : at + 2 * n_y] = jnp.concatenate(
                        [fluxes[i - 1][part], fluxes[i][part]], axis=0).astype(jnp.bfloat16)
        gram(old, j)

    @pl.when(g < n_z)
    def _():
        def step(j, carry):
            trip(j, True)
            return carry
        lax.fori_loop(0, groups, step, 0)
        value = jnp.zeros((n_x, n_y), jnp.float32)
        for phase in range(mob_ref.shape[0]):
            value = value + jnp.where(lab_ref[0] == phase, mob_ref[phase], jnp.float32(0.0))
        root = jnp.sqrt(value)
        root_ref[now] = root
        rootx_ref[0, 0:1] = root[:1]
        rootx_ref[0, 1:2] = root[n_x - 1 :]
        ok = (lanes < 4 * g + 4) & (lanes >= 4 * g)
        rooty_ref[...] = jnp.where(ok, pltpu.roll(root, 4 * g + 2, 1), rooty_ref[...])
        for side in range(2):
            rim_ref[0, side] = lines_ref[side].astype(jnp.bfloat16)

    @pl.when(g == n_z)
    def _():
        def step(j, carry):
            trip(j, False)
            return carry
        lax.fori_loop(0, groups, step, 0)
        for j in range(groups):
            gram(now, j)
        edge_ref[...] = side_ref[...].astype(jnp.bfloat16)

    for side in range(2):
        frim_ref[0, side] = lines_ref[2 + side].astype(jnp.bfloat16)


def gram_call(own, labels, mobility):
    vectors, n_z, n_x, n_y = own.shape
    order = vectors * ROWS
    blocks = n_x // ROWS
    groups = vectors // GROUP
    f32, bf16 = jnp.float32, jnp.bfloat16
    last = n_z - 1
    return pl.pallas_call(
        gram_kernel,
        grid=(n_z + 1,),
        in_specs=[
            pl.BlockSpec(memory_space=pltpu.SMEM),
            pl.BlockSpec((vectors, 1, n_x, n_y), lambda g: (0, jnp.minimum(g, last), 0, 0)),
            pl.BlockSpec((1, n_x, n_y), lambda g: (jnp.minimum(g, last), 0, 0)),
        ],
        out_specs=[
            pl.BlockSpec((order, order), lambda g: (0, 0)),
            pl.BlockSpec((1, 2, vectors, n_y), lambda g: (jnp.minimum(g, last), 0, 0, 0)),
            pl.BlockSpec((1, 2, vectors, n_y), lambda g: (jnp.maximum(g - 1, 0), 0, 0, 0)),
            pl.BlockSpec((vectors, n_x, n_y), lambda g: (0, 0, 0)),
            pl.BlockSpec((1, 2, n_y), lambda g: (jnp.minimum(g, last), 0, 0)),
            pl.BlockSpec((n_x, n_y), lambda g: (0, 0)),
        ],
        out_shape=[
            jax.ShapeDtypeStruct((order, order), f32),
            jax.ShapeDtypeStruct((n_z, 2, vectors, n_y), bf16),
            jax.ShapeDtypeStruct((n_z, 2, vectors, n_y), bf16),
            jax.ShapeDtypeStruct((vectors, n_x, n_y), bf16),
            jax.ShapeDtypeStruct((n_z, 2, n_y), f32),
            jax.ShapeDtypeStruct((n_x, n_y), f32),
        ],
        scratch_shapes=[
            pltpu.VMEM((2, vectors, n_x + 2 * ROWS, n_y), f32),
            pltpu.VMEM((vectors, n_x, n_y), f32),
            pltpu.VMEM((2, groups, order, blocks // groups * 2 * n_y), bf16),
            pltpu.VMEM((2, n_x, n_y), f32),
            pltpu.VMEM((4, vectors, n_y), f32),
            pltpu.VMEM((vectors, n_x, n_y), f32),
        ],
        compiler_params=pltpu.CompilerParams(vmem_limit_bytes=40 * 1024 * 1024),
    )(mobility, own, labels)


SLOTS = 21
MINOR = (((1,), (1,)), ((), ()))


def tile_kernel(acc_ref, frim_ref, edge_ref, rootx_ref, rooty_ref, xlow_ref, xupp_ref, ylow_ref, yupp_ref, out_ref,
                left_ref, right_ref, faces_ref, cut_ref):
    vectors, n_x, n_y = edge_ref.shape
    n_z = frim_ref.shape[0]
    order = acc_ref.shape[0]
    blocks = n_x // ROWS
    f32, bf16 = jnp.float32, jnp.bfloat16
    rows = lax.broadcasted_iota(jnp.int32, (n_x, n_y), 0)
    lanes = lax.broadcasted_iota(jnp.int32, (n_x, n_y), 1)
    spot = lanes % 4
    root = jnp.where((spot == 1) | (spot == 2), rooty_ref[...], 0.0)

    def pair_of(m, carry):
        kept = []
        for i in range(2):
            v = 2 * m + i
            own = edge_ref[v].astype(f32)
            near = jnp.where(lanes < 4, 0.0, pltpu.roll(own, 4, 1))
            near = near + jnp.where(lanes >= n_y - 4, 0.0, pltpu.roll(own, n_y - 4, 1))
            near = near + jnp.where(rows == 0, 0.0, pltpu.roll(own, 1, 0))
            near = near + jnp.where(rows == n_x - 1, 0.0, pltpu.roll(own, n_x - 1, 0))
            near = near + jnp.where(spot == 2, pltpu.roll(own, n_y - 1, 1), pltpu.roll(own, 1, 1))
            flux = (near - 6.0 * own) * root
            low = pltpu.roll(ylow_ref[v].astype(f32), 1, 1)
            upp = pltpu.roll(yupp_ref[v].astype(f32), n_y - 1, 1)
            over = jnp.where(spot == 2, low, upp) * root
            cut_ref[0, pl.ds(v, 1)] = over[:1]
            cut_ref[1, pl.ds(v, 1)] = over[n_x - 1 :]
            kept.append((flux, over, jnp.where(spot == 2, over, 0.0), jnp.where(spot == 1, over, 0.0)))
        for b in range(blocks):
            part = slice(b * ROWS, b * ROWS + ROWS)
            both = [jnp.concatenate([x[part], y[part]], axis=0).astype(bf16) for x, y in zip(*kept)]
            at = slice(b * n_y, b * n_y + n_y)
            first = pl.ds(pl.multiple_of(m * 2 * ROWS, 2 * ROWS), 2 * ROWS)
            second = pl.ds(pl.multiple_of(order + m * 2 * ROWS, 2 * ROWS), 2 * ROWS)
            left_ref[first, at] = both[0]
            left_ref[second, at] = both[1]
            right_ref[first, at] = both[2]
            right_ref[second, at] = both[3]
        return carry

    lax.fori_loop(0, vectors // 2, pair_of, 0)
    crossed = lax.dot_general(left_ref[...], right_ref[...], MINOR, preferred_element_type=f32)

    thin = lax.broadcasted_iota(jnp.int32, (vectors, n_y), 1)
    ends = []
    for side, halo_ref in enumerate((xlow_ref, xupp_ref)):
        total = jnp.zeros((vectors, n_y), f32)
        for z in range(n_z):
            over = halo_ref[z].astype(f32) * rootx_ref[z, side : side + 1]
            at = slice(z * n_y, z * n_y + n_y)
            faces_ref[side, :vectors, at] = frim_ref[z, side]
            faces_ref[side, vectors:, at] = over.astype(bf16)
            ok = (thin >= 4 * z) & (thin < 4 * z + 4)
            total = jnp.where(ok, pltpu.roll(over, (4 * z + 2) % n_y, 1), total)
        ends.append(total.astype(bf16))

    def put(slot, value):
        out_ref[:, slot * vectors : (slot + 1) * vectors] = value

    line = lax.broadcasted_iota(jnp.int32, (order, order), 0)
    column = lax.broadcasted_iota(jnp.int32, (order, order), 1)
    same = line % ROWS == column % ROWS
    pick = (lax.broadcasted_iota(jnp.int32, (order, vectors), 0) // ROWS
            == lax.broadcasted_iota(jnp.int32, (order, vectors), 1)).astype(f32)

    def fold(square):
        thick = jnp.where(same, square, 0.0).reshape(vectors, ROWS, order).sum(1)
        return lax.dot_general(thick, pick, (((1,), (0,)), ((), ())), precision=lax.Precision.HIGHEST,
                               preferred_element_type=f32)

    put(0, fold(acc_ref[...]))
    for side in range(2):
        gram = lax.dot_general(faces_ref[side], faces_ref[side], MINOR, preferred_element_type=f32)
        put(1 + 3 * side, gram[vectors:, :vectors])
        put(2 + 3 * side, gram[:vectors, vectors:])
        put(3 + 3 * side, gram[vectors:, vectors:])
        here = slice(side * order, side * order + order)
        cross = fold(crossed[:order, here])
        put(7 + 3 * side, cross.T)
        put(8 + 3 * side, cross)
        put(9 + 3 * side, fold(crossed[order:, here]))
    slot = 13
    for x in range(2):
        for y in range(2):
            along = jnp.where(thin % 4 == 2 - y, cut_ref[x], 0.0).astype(bf16)
            put(slot, lax.dot_general(along, ends[x], MINOR, preferred_element_type=f32))
            put(slot + 1, lax.dot_general(ends[x], along, MINOR, preferred_element_type=f32))
            slot += 2
    out_ref[:, SLOTS * vectors :] = jnp.zeros((vectors, out_ref.shape[1] - SLOTS * vectors), f32)


def tile_call(acc, frim, edge, rootx, rooty, xlow, xupp, ylow, yupp):
    vectors, n_x, n_y = edge.shape
    n_z = frim.shape[0]
    order = acc.shape[0]
    whole = pl.BlockSpec(memory_space=pltpu.VMEM)
    return pl.pallas_call(
        tile_kernel,
        in_specs=[whole] * 9,
        out_specs=whole,
        out_shape=jax.ShapeDtypeStruct((vectors, -(-SLOTS * vectors // n_y) * n_y), jnp.float32),
        scratch_shapes=[
            pltpu.VMEM((2 * order, n_x // ROWS * n_y), jnp.bfloat16),
            pltpu.VMEM((2 * order, n_x // ROWS * n_y), jnp.bfloat16),
            pltpu.VMEM((2, 2 * vectors, n_z * n_y), jnp.bfloat16),
            pltpu.VMEM((2, vectors, n_y), jnp.float32),
        ],
        compiler_params=pltpu.CompilerParams(vmem_limit_bytes=40 * 1024 * 1024),
    )(acc, frim, edge, rootx, rooty, xlow, xupp, ylow, yupp)


def local_tiles(own, labels, mobility_table):
    acc, rim, frim, edge, rootx, rooty = gram_call(own, labels, mobility_table)
    n_row = lax.axis_size("row")
    n_col = lax.axis_size("col")

    def up(values, axis, count):
        return lax.ppermute(values, axis, [(i, i + 1) for i in range(count - 1)])

    def down(values, axis, count):
        return lax.ppermute(values, axis, [(i + 1, i) for i in range(count - 1)])

    tiles = tile_call(
        acc, frim, edge, rootx, rooty,
        up(rim[:, 1], "row", n_row), down(rim[:, 0], "row", n_row),
        up(edge, "col", n_col), down(edge, "col", n_col),
    )
    vectors = own.shape[0]
    return tiles[:, : SLOTS * vectors].reshape(vectors, SLOTS, vectors).transpose(1, 2, 0)


def shift_grid(values, offset):
    widths = [(1, 1), (1, 1)] + [(0, 0)] * (values.ndim - 2)
    padded = jnp.pad(values, widths)
    start_x = 1 - offset[0]
    start_y = 1 - offset[1]
    return padded[start_x : start_x + values.shape[0], start_y : start_y + values.shape[1]]


def to_owner(stack, n_row, n_col):
    slots = stack.shape[0]
    vectors = stack.shape[1]
    row_blocks = vectors // (NB * n_row)
    col_blocks = vectors // (NB * n_col)
    split = stack.reshape(slots, row_blocks, n_row, NB, col_blocks, n_col, NB)
    moved = split.transpose(2, 5, 0, 4, 6, 1, 3)
    return moved.reshape(n_row, n_col, slots * col_blocks * NB * row_blocks * NB)


def place_bands(bands, n_row, n_col):
    n_sub = n_row * n_col
    sub_x = jnp.arange(n_sub, dtype=jnp.int32) // n_col
    sub_y = jnp.arange(n_sub, dtype=jnp.int32) % n_col
    total = None
    for index in range(9):
        step_x = index // 3 - 1
        step_y = index % 3 - 1
        match = (
            (sub_x[:, None] == sub_x[None, :] + step_x)
            & (sub_y[:, None] == sub_y[None, :] + step_y)
        ).astype(jnp.float32)
        flat = bands[index].reshape(n_sub, -1).T
        term = match[:, None, :] * flat[None, :, :]
        total = term if total is None else total + term
    return total


def body(geneo_vectors, phase_labels, phase_mobility):
    vectors = geneo_vectors.shape[0]
    n_row = lax.axis_size("row")
    n_col = lax.axis_size("col")
    n_sub = n_row * n_col
    row_blocks = vectors // (NB * n_row)
    col_blocks = vectors // (NB * n_col)
    rows_here = row_blocks * NB * n_sub
    piece_len = col_blocks * NB * row_blocks * NB
    width = PSUB * vectors
    tiles = local_tiles(geneo_vectors, phase_labels, phase_mobility)
    offsets = slot_offsets()
    routed = lax.all_to_all(
        lax.all_to_all(
            to_owner(tiles, n_row, n_col), "row", split_axis=0, concat_axis=0, tiled=True
        ),
        "col",
        split_axis=1,
        concat_axis=1,
        tiled=True,
    )
    routed = routed.reshape(n_row, n_col, len(offsets), piece_len)
    bands = [jnp.zeros((n_row, n_col, piece_len), jnp.float32) for count in range(9)]
    for slot, pair_off in enumerate(offsets):
        place = band_index(pair_off[0], pair_off[1])
        bands[place] = bands[place] + shift_grid(routed[:, :, slot], pair_off[0])
    local = place_bands(bands, n_row, n_col).reshape(n_sub, col_blocks * NB, rows_here)
    row_index = lax.axis_index("row")
    col_index = lax.axis_index("col")
    row_sub = jnp.arange(rows_here, dtype=jnp.int32) % n_sub
    ends = 2 * PSUB
    mine = local[:ends].reshape(ends, col_blocks, NB, rows_here)
    parts = lax.all_gather(mine, ("row", "col"), axis=0, tiled=False)
    parts = parts.reshape(n_row, n_col, ends, col_blocks, NB, rows_here)
    panels = parts.transpose(2, 3, 1, 4, 0, 5).reshape(2, width, n_row, rows_here)

    def rows_of(block, first, last):
        grid = block.reshape(width, n_row, row_blocks, NB, n_sub)[..., first:last]
        return grid.transpose(0, 4, 2, 1, 3).reshape(width, (last - first) * vectors)

    done = []
    for panel in range(2):
        first = panel * PSUB
        last = first + PSUB
        block = panels[panel]
        for solved in done:
            change = lax.dot_general(
                rows_of(solved, first, last),
                solved.reshape(width, n_row * rows_here),
                (((0,), (0,)), ((), ())),
                precision=lax.Precision.HIGHEST,
                preferred_element_type=jnp.float32,
            )
            block = block - change.reshape(width, n_row, rows_here)
        block = jnp.where(row_sub >= first, block, jnp.float32(0.0))
        low = jnp.linalg.cholesky(rows_of(block, first, last).T)
        solved = lax.linalg.triangular_solve(
            low, block.reshape(width, n_row * rows_here), left_side=True, lower=True
        ).reshape(width, n_row, rows_here)
        done.append(solved)
    both = jnp.concatenate(done, axis=0)
    rows_mine = lax.dynamic_index_in_dim(both, row_index, 1, keepdims=False)
    by_block = both.reshape(2 * width, n_row, row_blocks, NB, n_sub).transpose(0, 2, 1, 3, 4)
    picked = lax.dynamic_index_in_dim(
        by_block.reshape(2 * width, row_blocks, n_row // n_col, n_col, NB, n_sub),
        col_index,
        3,
        keepdims=False,
    )
    columns = (
        picked.reshape(2 * width, col_blocks * NB, n_sub)
        .transpose(0, 2, 1)
        .reshape(2 * width, n_sub * col_blocks * NB)
    )
    update = lax.dot_general(
        columns,
        rows_mine,
        (((0,), (0,)), ((), ())),
        precision=lax.Precision.HIGHEST,
        preferred_element_type=jnp.float32,
    ).reshape(n_sub, col_blocks * NB, rows_here)
    panel_mine = lax.dynamic_index_in_dim(
        rows_mine.reshape(ends, col_blocks, n_col, NB, rows_here), col_index, 2, keepdims=False
    ).reshape(ends, col_blocks * NB, rows_here)
    rest = jnp.where(row_sub < ends, jnp.float32(0.0), local[ends:] - update[ends:])
    local = jnp.concatenate([panel_mine, rest], axis=0)
    return local.reshape(n_sub, col_blocks, 1, NB, row_blocks, 1, NB, n_sub)


def solution(mesh):
    return jax.shard_map(
        body,
        mesh=mesh,
        in_specs=(P(None, None, "row", "col"), P(None, "row", "col"), P()),
        out_specs=P(None, None, "col", None, None, "row", None, None),
        check_vma=False,
    )
```

time: 460 us -> 177 us (0.38)
  Pallas kernels: 185 us -> 55.8 us
  local copies, waits for them, and re-layouts: 139 us -> 11.7 us
  other arithmetic: 44.9 us -> 26.8 us
  matrix products: 12.4 us -> 1.48 us
  waiting for transfers between devices: 10.8 us -> 19.8 us
    pallas_call x1 -> x2, Pallas kernels: 185 us -> 55.8 us  [the longest x1 52 us: gram_call(): pl.pallas_call(gram_kernel, grid=(n_z + 1,), in_specs=[pl.BlockSpec(memor...]
    another operation x41 -> x0, local copies, waits for them, and re-layouts: 98.4 us -> none  [the longest x39 97.4 us: local_tiles(): return jnp.stack(tiles)]
    slice x13 -> x0, local copies, waits for them, and re-layouts: 17.3 us -> none  [the longest x2 3.7 us: flux_gram(): own_edge = edges[:, :, half:half + 2 * n_z].reshape(vectors, n_x, n_z, 2)]
    dot_general x12 -> x0, matrix products: 10.9 us -> none  [contract_cells(): lax.dot_general(flat_left, flat_right, (((1,), (1,)), ((), ())), preferre...]
    ppermute x4, waiting for transfers between devices: 0.01 us -> 8.5 us  [the longest x2 4.69 us: down(): return lax.ppermute(values, axis, [(i + 1, i) for i in range(count - 1)])]
    convert_element_type x7 -> x0, other arithmetic: 8.05 us -> none  [the longest x4 4.82 us: local_tiles(): across = (layer_z.astype(jnp.float32) * layer_r).astype(jnp.bfloat16)]
    unnamed x27 -> x5, local copies, waits for them, and re-layouts: 6.83 us -> 1.89 us
  transfers between devices with their start and end apart: 6 -> 6, of which waited for: 2 -> 4; matrix products, arithmetic and copies ran while one was open for 19% -> 0% of each run, Pallas kernels for 41% -> 0%
where the time goes in v1:
time: 177 us; the launch traced here: 176 us
  Pallas kernels  55.8 us (32%)
  blocking collectives  38.7 us (22%)
  other arithmetic  26.8 us (15%)
  starting transfers between devices  21.5 us (12%)
  waiting for transfers between devices  19.8 us (11%)
  local copies, waits for them, and re-layouts  11.7 us (7%)
    pallas_call x1, Pallas kernels, gram_call(): pl.pallas_call(gram_kernel, grid=(n_z + 1,), in_specs=[pl.BlockSpec(memor...  52 us
    all_gather x1, blocking collectives, body(): parts = lax.all_gather(mine, ('row', 'col'), axis=0, tiled=False)  38.7 us
    another operation x6, other arithmetic, body(): low = jnp.linalg.cholesky(rows_of(block, first, last).T)  13 us
    another operation x4, other arithmetic, body(): lax.linalg.triangular_solve(low, block.reshape(width, n_row * rows_here),...  11.1 us
    all_to_all x1, starting transfers between devices, body(): lax.all_to_all(to_owner(tiles, n_row, n_col), 'row', split_axis=0, concat...  9 us
    all_to_all x1, waiting for transfers between devices, body(): lax.all_to_all(to_owner(tiles, n_row, n_col), 'row', split_axis=0, concat...  7.1 us
    ppermute x2, starting transfers between devices, up(): return lax.ppermute(values, axis, [(i, i + 1) for i in range(count - 1)])  6.66 us
    ppermute x2, waiting for transfers between devices, down(): return lax.ppermute(values, axis, [(i + 1, i) for i in range(count - 1)])  4.69 us
  transfers between devices with their start and end apart: 6, of which 4 were waited for; matrix products, arithmetic and copies ran while one was open for 0% of the time, Pallas kernels for 0%

profile of v1, /device:TPU:0, one launch (start us, length us, event | category | flops | bytes accessed | tf_op | source)
XLA Modules:
  0.0 176.4 jit_solution(106391391254238839)
XLA Ops:
  0.0 1.2 copy-done
  1.2 0.7 copy-done.1
  1.9 52.0 %shard_map.37 = (f32[256,256]{1,0:T(8,128)S(1)}, bf16[32,2,32,128]{3,2,1,0:T(8,128)(2,1)S(1)}, bf16[32,2,32,128]{3,2,1,0:T(8,128)(2,1)S(1)}, bf16[32,64,128]{2,1...) custom-call(f32[4]{0:T(128)S(1)} %copy-done.1, bf16[32,32,64,128]{3,2,1,0:T(8,128)(2,1)} %own_ref.1, ...), custom_call_target="tpu_custom_call" | custom-call | tf_op jit(solution)/shard_map/pallas_call | solution.py:137
  53.9 2.4 %collective-permute-start.2 = (bf16[32,64,128]{2,1,0:T(8,128)(2,1)S(1)}, bf16[32,64,128]{2,1,0:T(8,128)(2,1)S(1)}, u32[]{:S(2)}, u32[]{:S(2)}) collective-permute-start(bf16[32,64,128]{2,1,0:T(8,128)(2,1)S(1)} %get-tuple-element.15.edge_ref), channel_id=1, source_target_pairs={{0,1},{1,2},{2,3},{4,5},{5,6},{6,7},{8,9},{9,10},{10,11},{12,13},{... | collective-permute-start | bytes 1572872 | tf_op jit(solution)/shard_map/ppermute | solution.py:295
  56.3 1.3 collective-permute-start.3
  57.6 4.2 %collective-permute-start = (bf16[32,32,128]{2,1,0:T(8,128)(2,1)S(1)}, bf16[32,32,128]{2,1,0:T(8,128)(2,1)S(1)}, u32[]{:S(2)}, u32[]{:S(2)}) collective-permute-start(bf16[32,32,128]{2,1,0:T(8,128)(2,1)S(1)} %get-tuple-element.22), channel_id=1, source_target_pairs={{0,4},{4,8},{8,12},{12,16},{16,20},{20,24},{24,28},{1,5},{5,9},{9,... | collective-permute-start | bytes 786440 | tf_op jit(solution)/shard_map/ppermute | solution.py:295
  61.9 1.3 collective-permute-start.1
  63.2 0.1 fusion.32
  63.3 3.8 %collective-permute-done.xlow_ref = bf16[32,32,128]{2,1,0:T(8,128)(2,1)S(1)} collective-permute-done((bf16[32,32,128]{2,1,0:T(8,128)(2,1)S(1)}, bf16[32,32,128]{2,1,0:T(8,128)(2,1)S(1)}, u32[]{:S(2)}, u32[]{:S(2)}) %collective-permute-start) | collective-permute-done | bytes 262176 | tf_op jit(solution)/shard_map/ppermute | solution.py:295
  67.1 4.7 %collective-permute-done.1.xupp_ref = bf16[32,32,128]{2,1,0:T(8,128)(2,1)S(1)} collective-permute-done((bf16[32,32,128]{2,1,0:T(8,128)(2,1)S(1)}, bf16[32,32,128]{2,1,0:T(8,128)(2,1)S(1)}, u32[]{:S(2)}, u32[]{:S(2)}) %collective-permute-start.1) | collective-permute-done | bytes 262176 | tf_op jit(solution)/shard_map/ppermute | solution.py:298
  71.8 0.0 collective-permute-done.2.ylow_ref
  71.8 0.0 collective-permute-done.3.yupp_ref
  71.8 3.8 %shard_map.38 = f32[32,768]{1,0:T(8,128)S(1)} custom-call(f32[256,256]{1,0:T(8,128)S(1)} %get-tuple-element.13.acc_ref, bf16[32,2,32,128]{3,2,1,0:T(8,128)(2,1)S(1)} %get-tuple-element.14.frim_ref, bf16[32,64,128]{2,1,0:T(8,128)(2,1)S(1)} %get-tuple-element.15.edge_ref, f32[32,2,128]{2,1,0:T(2,128)S(1)} %get-tuple-element.16.rootx_ref, ...), custom_call_target="tpu_custom_call" | custom-call | tf_op jit(solution)/shard_map/pallas_call | solution.py:274
  75.7 0.1 reshape.632
  75.8 0.5 copy.126
  76.4 2.3 %copy.127 = f32[8,4,21,4,2,2,2]{0,6,5,4,3,2,1:T(2,128)S(1)} copy(f32[8,4,21,4,2,2,2]{2,4,1,3,6,0,5:T(2,128)S(1)} %bitcast.183) | data formatting | bytes 172032 | tf_op jit(solution)/shard_map/transpose | solution.py:323
  78.7 1.1 copy.128
  79.8 9.0 %all-to-all-start = ((f32[8,4,672]{2,1,0:T(4,128)}), f32[8,4,672]{2,1,0:T(4,128)S(1)}, u32[]{:S(2)}, u32[]{:S(2)}) async-start(f32[8,4,672]{2,1,0:T(4,128)} %copy.128), calls=%async_computation | async-start | bytes 196608 | tf_op jit(solution)/shard_map/all_to_all | solution.py:358
  88.8 7.1 %all-to-all-done = f32[8,4,672]{2,1,0:T(4,128)S(1)} async-done(((f32[8,4,672]{2,1,0:T(4,128)}), f32[8,4,672]{2,1,0:T(4,128)S(1)}, u32[]{:S(2)}, u32[]{:S(2)}) %all-to-all-start) | async-done | bytes 86048 | tf_op jit(solution)/shard_map/all_to_all | solution.py:358
  95.9 0.7 copy.129
  96.6 3.3 %all-to-all-start.1 = ((f32[8,4,672]{2,0,1:T(8,128)}), f32[8,4,672]{2,0,1:T(8,128)S(1)}, u32[]{:S(2)}, u32[]{:S(2)}) async-start(f32[8,4,672]{2,0,1:T(8,128)} %copy.129), calls=%async_computation.1 | async-start | bytes 196608 | tf_op jit(solution)/shard_map/all_to_all | solution.py:357
  99.9 4.2 %all-to-all-done.1 = f32[8,4,672]{2,0,1:T(8,128)S(1)} async-done(((f32[8,4,672]{2,0,1:T(8,128)}), f32[8,4,672]{2,0,1:T(8,128)S(1)}, u32[]{:S(2)}, u32[]{:S(2)}) %all-to-all-start.1) | async-done | bytes 86048 | tf_op jit(solution)/shard_map/all_to_all | solution.py:357
  104.1 0.1 reshape.635
  104.3 0.3 fusion.43
  104.6 0.1 copy.159
  104.7 0.1 copy.156
  104.8 0.1 copy.153
  104.9 0.1 copy.150
  105.0 0.1 copy.147
  105.1 0.1 copy.141
  105.2 0.1 copy.138
  105.3 0.1 copy.135
  105.4 0.1 copy.132
  105.5 0.3 multiply_add_fusion
  105.8 0.1 all_gather_reshape.3
  105.9 38.7 %all_gather.3 = f32[32,4,4,2,128]{4,2,3,1,0:T(4,128)S(1)} all-gather(f32[1,4,4,2,128]{4,2,3,1,0:T(4,128)S(1)} %copy.160), channel_id=1, replica_groups=mesh['row'=8,'col'=4] {'row','col'}, dimensions={0}, use_global_device_ids=true | all-gather | bytes 540672 | tf_op jit(solution)/shard_map/all_gather | solution.py:377
  144.6 0.3 copy.161
  145.0 0.8 squeeze.108
  145.9 0.5 fusion.1
  146.4 0.9 copy.163
  147.3 0.1 copy.164
  147.4 5.8 %cholesky.44 = f32[64,64]{1,0:T(8,128)S(1)} custom-call(f32[64,64]{1,0:T(8,128)S(1)} %add_multiply_fusion.1), custom_call_target="Cholesky" | custom-call | tf_op jit(solution)/shard_map/jit(cholesky)/cholesky | solution.py:400
  153.3 0.6 compare_reduce_fusion.1
  153.9 0.7 fusion.16
  154.6 4.9 %custom-call.6 = f32[1,64,64]{1,2,0:T(8,128)S(1)} custom-call(f32[1,64,64]{2,1,0:T(8,128)S(1)} %fusion.16), custom_call_target="InvertDiagBlocksLowerTriangular" | custom-call | tf_op jit(solution)/shard_map/triangular_solve/custom-call.0 | solution.py:401
  159.5 0.4 fusion.3
  159.9 0.2 copy.168
  160.1 0.2 copy.167
  160.4 0.4 fusion
  160.8 0.2 copy.171
  161.0 0.1 copy.173
  161.1 5.8 %cholesky.55 = f32[64,64]{1,0:T(8,128)S(1)} custom-call(f32[64,64]{1,0:T(8,128)S(1)} %add_multiply_fusion), custom_call_target="Cholesky" | custom-call | tf_op jit(solution)/shard_map/jit(cholesky)/cholesky | solution.py:400
  167.0 0.6 compare_reduce_fusion
  167.7 0.7 fusion.17
  168.3 4.9 %custom-call.7 = f32[1,64,64]{1,2,0:T(8,128)S(1)} custom-call(f32[1,64,64]{2,1,0:T(8,128)S(1)} %fusion.17), custom_call_target="InvertDiagBlocksLowerTriangular" | custom-call | tf_op jit(solution)/shard_map/triangular_solve/custom-call.0 | solution.py:401
  173.2 0.4 fusion.5
  173.7 0.2 copy.178
  173.9 0.2 pad_maximum_fusion
  174.1 0.1 copy.219
  174.2 0.2 fusion.12
  174.5 0.4 slice.213
  174.9 0.1 concatenate.15
  175.0 0.3 fusion.2
  175.4 1.1 pad_maximum_fusion.1
  (48 shorter events, 0.6 us)
Async XLA Ops:
  0.0 1.2 copy-start
  1.2 0.7 copy-start.1
  53.9 18.0 %collective-permute-start.2 = (bf16[32,64,128]{2,1,0:T(8,128)(2,1)S(1)}, bf16[32,64,128]{2,1,0:T(8,128)(2,1)S(1)}, u32[]{:S(2)}, u32[]{:S(2)}) collective-permute-start(bf16[32,64,128]{2,1,0:T(8,128)(2,1)S(1)} %get-tuple-element.15.edge_ref), channel_id=1, source_target_pairs={{0,1},{1,2},{2,3},{4,5},{5,6},{6,7},{8,9},{9,10},{10,11},{12,13},{... | collective-permute-start | bytes 1572872 | tf_op jit(solution)/shard_map/ppermute | solution.py:295
  56.3 15.5 %collective-permute-start.3 = (bf16[32,64,128]{2,1,0:T(8,128)(2,1)S(1)}, bf16[32,64,128]{2,1,0:T(8,128)(2,1)S(1)}, u32[]{:S(2)}, u32[]{:S(2)}) collective-permute-start(bf16[32,64,128]{2,1,0:T(8,128)(2,1)S(1)} %get-tuple-element.15.edge_ref), channel_id=1, source_target_pairs={{1,0},{2,1},{3,2},{5,4},{6,5},{7,6},{9,8},{10,9},{11,10},{13,12},{... | collective-permute-start | bytes 1572872 | tf_op jit(solution)/shard_map/ppermute | solution.py:298
  57.6 9.5 %collective-permute-start = (bf16[32,32,128]{2,1,0:T(8,128)(2,1)S(1)}, bf16[32,32,128]{2,1,0:T(8,128)(2,1)S(1)}, u32[]{:S(2)}, u32[]{:S(2)}) collective-permute-start(bf16[32,32,128]{2,1,0:T(8,128)(2,1)S(1)} %get-tuple-element.22), channel_id=1, source_target_pairs={{0,4},{4,8},{8,12},{12,16},{16,20},{20,24},{24,28},{1,5},{5,9},{9,... | collective-permute-start | bytes 786440 | tf_op jit(solution)/shard_map/ppermute | solution.py:295
  61.9 9.9 %collective-permute-start.1 = (bf16[32,32,128]{2,1,0:T(8,128)(2,1)S(1)}, bf16[32,32,128]{2,1,0:T(8,128)(2,1)S(1)}, u32[]{:S(2)}, u32[]{:S(2)}) collective-permute-start(bf16[32,32,128]{2,1,0:T(8,128)(2,1)S(1)} %get-tuple-element.21), channel_id=1, source_target_pairs={{4,0},{8,4},{12,8},{16,12},{20,16},{24,20},{28,24},{5,1},{9,5},{13... | collective-permute-start | bytes 786440 | tf_op jit(solution)/shard_map/ppermute | solution.py:298
  79.8 16.1 %all-to-all-start = ((f32[8,4,672]{2,1,0:T(4,128)}), f32[8,4,672]{2,1,0:T(4,128)S(1)}, u32[]{:S(2)}, u32[]{:S(2)}) async-start(f32[8,4,672]{2,1,0:T(4,128)} %copy.128), calls=%async_computation | async-start | bytes 196608 | tf_op jit(solution)/shard_map/all_to_all | solution.py:358
  96.6 7.6 %all-to-all-start.1 = ((f32[8,4,672]{2,0,1:T(8,128)}), f32[8,4,672]{2,0,1:T(8,128)S(1)}, u32[]{:S(2)}, u32[]{:S(2)}) async-start(f32[8,4,672]{2,0,1:T(8,128)} %copy.129), calls=%async_computation.1 | async-start | bytes 196608 | tf_op jit(solution)/shard_map/all_to_all | solution.py:357

commit v2 on v1

--- a/solution.py
+++ b/solution.py
@@ -1,3 +1,5 @@
+import functools
+
 import jax
 import jax.numpy as jnp
 from jax import lax
@@ -7,24 +9,9 @@
 
 NB = 2
 PSUB = 2
-
-
-FACES = ((-1, 0), (1, 0), (0, -1), (0, 1))
-
-
-def slot_offsets():
-    offsets = [((0, 0), (0, 0))]
-    for face in FACES:
-        offsets += [((0, 0), face), (face, (0, 0)), (face, face)]
-    for face_x in FACES[:2]:
-        for face_y in FACES[2:]:
-            offsets += [(face_x, face_y), (face_y, face_x)]
-    return offsets
-
-
-def band_index(from_off, to_off):
-    return (to_off[0] - from_off[0] + 1) * 3 + (to_off[1] - from_off[1] + 1)
-
+SLOTS = 21
+MESH = pl.DeviceIdType.MESH
+PLAIN = (((1,), (0,)), ((), ()))
 
 ROWS = 8
 GROUP = 8
@@ -170,7 +157,6 @@
     )(mobility, own, labels)
 
 
-SLOTS = 21
 MINOR = (((1,), (1,)), ((), ()))
 
 
@@ -266,7 +252,7 @@
     out_ref[:, SLOTS * vectors :] = jnp.zeros((vectors, out_ref.shape[1] - SLOTS * vectors), f32)
 
 
-def tile_call(acc, frim, edge, rootx, rooty, xlow, xupp, ylow, yupp):
+def tile_call(acc, frim, edge, rootx, rooty, xlow, xupp, ylow, yupp, n_col):
     vectors, n_x, n_y = edge.shape
     n_z = frim.shape[0]
     order = acc.shape[0]
@@ -275,7 +261,7 @@
         tile_kernel,
         in_specs=[whole] * 9,
         out_specs=whole,
-        out_shape=jax.ShapeDtypeStruct((vectors, -(-SLOTS * vectors // n_y) * n_y), jnp.float32),
+        out_shape=jax.ShapeDtypeStruct((vectors, -(-SLOTS // n_col) * n_col * vectors), jnp.float32),
         scratch_shapes=[
             pltpu.VMEM((2 * order, n_x // ROWS * n_y), jnp.bfloat16),
             pltpu.VMEM((2 * order, n_x // ROWS * n_y), jnp.bfloat16),
@@ -286,10 +272,278 @@
     )(acc, frim, edge, rootx, rooty, xlow, xupp, ylow, yupp)
 
 
-def local_tiles(own, labels, mobility_table):
-    acc, rim, frim, edge, rootx, rooty = gram_call(own, labels, mobility_table)
+FACES = ((-1, 0), (1, 0), (0, -1), (0, 1))
+
+
+def slot_offsets():
+    offsets = [((0, 0), (0, 0))]
+    for face in FACES:
+        offsets += [((0, 0), face), (face, (0, 0)), (face, face)]
+    for face_x in FACES[:2]:
+        for face_y in FACES[2:]:
+            offsets += [(face_x, face_y), (face_y, face_x)]
+    return offsets
+
+
+def exact_dot(left, right, dims=PLAIN):
+    return lax.dot_general(left, right, dims, precision=lax.Precision.HIGHEST, preferred_element_type=jnp.float32)
+
+
+def swap_bits(tiles, bits):
+    lanes = lax.broadcasted_iota(jnp.int32, tiles[0].shape, 1)
+    width = tiles[0].shape[1]
+    for index, lane in bits:
+        low = lanes // lane % 2 == 0
+        out = list(tiles)
+        for i in range(len(tiles)):
+            if i // index % 2 == 0:
+                a, b = tiles[i], tiles[i + index]
+                out[i] = jnp.where(low, a, pltpu.roll(b, lane, 1))
+                out[i + index] = jnp.where(low, pltpu.roll(a, width - lane, 1), b)
+        tiles = out
+    return tiles
+
+
+def powers(count):
+    return [1 << i for i in range(count.bit_length() - 1)]
+
+
+def trade_kernel(n_row, n_col, tile_ref, out_ref, all_ref, send_ref, mine_ref, here_ref,
+                 send_sem, recv_sem, send_sem2, recv_sem2):
+    vectors = tile_ref.shape[0]
+    n_sub = n_row * n_col
+    col_blocks = vectors // (NB * n_col)
+    width = n_col * vectors
+    depth = col_blocks * NB
+    r = lax.axis_index("row")
+    c = lax.axis_index("col")
+    me = r * n_col + c
+
+    def peer(k):
+        other = lax.rem(me + k, n_sub)
+        return other, (other // n_col, lax.rem(other, n_col))
+
+    barrier = pltpu.get_barrier_semaphore()
+
+    def greet(k, carry):
+        pl.semaphore_signal(barrier, inc=1, device_id=peer(k)[1], device_id_type=MESH)
+        return carry
+
+    lax.fori_loop(1, n_sub, greet, 0)
+
+    at = lax.broadcasted_iota(jnp.int32, (vectors, vectors), 0)
+    source = (at // NB % col_blocks * n_col + at // (NB * col_blocks)) * NB + at % NB
+    turn = (source == lax.broadcasted_iota(jnp.int32, (vectors, vectors), 1)).astype(jnp.float32)
+    ordered = exact_dot(turn, tile_ref[...])
+    packs = tile_ref.shape[1] // width
+    blank = jnp.zeros((depth, width), jnp.float32)
+    for column in range(n_col):
+        some = slice(column * depth, column * depth + depth)
+        tiles = [ordered[some, k * width : k * width + width] if k < packs else blank for k in range(n_row)]
+        tiles = swap_bits(tiles, [(bit, NB * bit) for bit in powers(n_row)])
+        for row in range(n_row):
+            send_ref[row * n_col + column] = tiles[row]
+    pl.semaphore_wait(barrier, n_sub - 1)
+
+    def exchange(kind, source_of, target_ref, sends, recvs):
+        def copy(k):
+            other, where = peer(k)
+            return pltpu.make_async_remote_copy(
+                src_ref=source_of(other), dst_ref=target_ref.at[me], send_sem=sends.at[other], recv_sem=recvs.at[me],
+                device_id=where, device_id_type=MESH)
+
+        def begin(k, carry):
+            copy(k).start()
+            return carry
+
+        lax.fori_loop(1, n_sub, begin, 0)
+
+        def finish(k, carry):
+            other, where = peer(k)
+            pltpu.make_async_remote_copy(
+                src_ref=source_of(other), dst_ref=target_ref.at[other], send_sem=sends.at[other],
+                recv_sem=recvs.at[other], device_id=where, device_id_type=MESH).wait_recv()
+            return carry
+
+        lax.fori_loop(1, n_sub, finish, 0)
+
+        def drain(k, carry):
+            copy(k).wait_send()
+            return carry
+
+        lax.fori_loop(1, n_sub, drain, 0)
+
+    here_ref[me] = send_ref[me]
+    exchange("tiles", lambda other: send_ref.at[other], here_ref, send_sem, recv_sem)
+
+    tiles = [here_ref[s] for s in range(n_sub)]
+    quads = n_sub // n_row
+    bits = [(bit, NB * bit) for bit in powers(n_row)]
+    bits += [(n_row * bit, vectors * bit) for bit in powers(quads)]
+    tiles = swap_bits(tiles, bits)
+    offsets = slot_offsets()
+    stack = jnp.concatenate([tiles[slot % quads * n_row + slot // quads] for slot in range(SLOTS)], axis=0)
+    into = lax.broadcasted_iota(jnp.int32, (width, width), 1)
+    sub, tru = into % n_sub, into // n_sub
+    origin = sub // n_row * vectors + (tru // NB * n_row + sub % n_row) * NB + tru % NB
+    order = (origin == lax.broadcasted_iota(jnp.int32, (width, width), 0)).astype(jnp.float32)
+    stack = exact_dot(stack, order)
+    bands = {}
+    for slot, (start, stop) in enumerate(offsets):
+        value = stack[slot * depth : slot * depth + depth]
+        shift = start[0] * n_col + start[1]
+        if shift:
+            value = pltpu.roll(value, shift % width, 1)
+        step = (stop[0] - start[0]) * n_col + stop[1] - start[1]
+        bands[step] = bands[step] + value if step in bands else value
+    lanes = lax.broadcasted_iota(jnp.int32, (depth, width), 1) % n_sub
+    ends = 2 * PSUB
+    reach = 2 * n_col
+    packed = jnp.zeros((depth, width), jnp.float32)
+    for b in range(n_sub):
+        value = jnp.zeros((depth, width), jnp.float32)
+        for step, band in bands.items():
+            if 0 <= b - step < n_sub:
+                value = jnp.where(lanes == b - step, band, value)
+        out_ref[b] = value
+        if b < ends:
+            value = jnp.where(lanes < reach, value, 0.0)
+            packed = packed + (pltpu.roll(value, reach * b, 1) if b else value)
+    mine_ref[...] = packed
+    all_ref[me] = packed
+    exchange("panel", lambda other: mine_ref, all_ref, send_sem2, recv_sem2)
+
+
+def trade_call(tiles, n_row, n_col):
+    vectors = tiles.shape[0]
+    n_sub = n_row * n_col
+    depth = vectors // n_col
+    width = vectors // n_row * n_sub
+    f32 = jnp.float32
+    whole = pl.BlockSpec(memory_space=pltpu.VMEM)
+    return pl.pallas_call(
+        functools.partial(trade_kernel, n_row, n_col),
+        in_specs=[whole],
+        out_specs=[whole, whole],
+        out_shape=[jax.ShapeDtypeStruct((n_sub, depth, width), f32), jax.ShapeDtypeStruct((n_sub, depth, width), f32)],
+        scratch_shapes=[
+            pltpu.VMEM((n_sub, depth, width), f32),
+            pltpu.VMEM((depth, width), f32),
+            pltpu.VMEM((n_sub, depth, width), f32),
+            pltpu.SemaphoreType.DMA((n_sub,)),
+            pltpu.SemaphoreType.DMA((n_sub,)),
+            pltpu.SemaphoreType.DMA((n_sub,)),
+            pltpu.SemaphoreType.DMA((n_sub,)),
+        ],
+        compiler_params=pltpu.CompilerParams(collective_id=0, has_side_effects=True,
+                                             vmem_limit_bytes=24 * 1024 * 1024),
+    )(tiles)
+
+
+def panel_kernel(n_row, n_col, local_ref, all_ref, out_ref, low_ref):
+    n_sub, depth, width = local_ref.shape
+    vectors = depth * n_col
+    ends, reach = 2 * PSUB, 2 * n_col
+    f32 = jnp.float32
+    r = lax.axis_index("row")
+    c = lax.axis_index("col")
+    order = ends * vectors
+    at = lax.broadcasted_iota(jnp.int32, (vectors, vectors), 1)
+    col_blocks = depth // NB
+    source = (at // NB % col_blocks * n_col + at // (NB * col_blocks)) * NB + at % NB
+    turn = (source == lax.broadcasted_iota(jnp.int32, (vectors, vectors), 0)).astype(f32)
+    high = reach // ends
+    by_column = []
+    for column in range(n_col):
+        tiles = [all_ref[row * n_col + column] for row in range(n_row)]
+        bits = [(bit, ends * bit) for bit in powers(n_row)]
+        by_column.append(swap_bits(tiles, bits))
+    halves = []
+    for h in range(high):
+        parts = []
+        for b in range(ends):
+            parts.append(exact_dot(turn, jnp.concatenate([by_column[column][b * high + h] for column in range(n_col)], axis=0)))
+        halves.append(jnp.concatenate(parts, axis=0))
+    tall = 8
+    count = order // tall
+    work = [[halves[h][t * tall : t * tall + tall] for t in range(count)] for h in range(high)]
+    for k in range(order):
+        t, s = divmod(k, tall)
+        b, q = divmod(k, vectors)
+        tr, row, u = q // (NB * n_row), q // NB % n_row, q % NB
+        lane = (tr * NB + u) * n_sub + row * ends + b
+        rows = [work[h][t][s : s + 1] for h in range(high)]
+        pivot = rows[0][:, lane : lane + 1]
+        scale = lax.rsqrt(pivot)
+        scaled = [x * scale for x in rows]
+        for h in range(high):
+            low_ref[k : k + 1, h * width : h * width + width] = scaled[h]
+        for i in range(t, count):
+            weight = work[0][i][:, lane : lane + 1] * scale
+            for h in range(high):
+                work[h][i] = work[h][i] - weight * scaled[h]
+    shape = (order, high * width)
+    lane = lax.broadcasted_iota(jnp.int32, shape, 1)
+    inner = lane % width
+    a = lane // width * ends + inner % ends
+    p = (inner // (NB * n_sub) * n_row + inner % n_sub // ends) * NB + inner // n_sub % NB
+    keep = a * vectors + p >= lax.broadcasted_iota(jnp.int32, shape, 0)
+    low = jnp.where(keep, low_ref[...], 0.0)
+
+    shape = (high * width, width)
+    lane = lax.broadcasted_iota(jnp.int32, shape, 0)
+    goal = lax.broadcasted_iota(jnp.int32, shape, 1)
+    inner = lane % width
+    a = lane // width * ends + inner % ends
+    mine = (inner % n_sub // ends == r) & (inner // n_sub == goal // n_sub) & (a == goal % n_sub)
+    rows_mine = exact_dot(low, mine.astype(f32))
+    shape = (ends * depth, order)
+    goal = lax.broadcasted_iota(jnp.int32, shape, 0)
+    lane = lax.broadcasted_iota(jnp.int32, shape, 1)
+    b, inner = goal // depth, goal % depth
+    q = (inner // NB * n_col + c) * NB + inner % NB
+    pick = (lane == b * vectors + q).astype(f32)
+    panel = exact_dot(pick, rows_mine)
+    for b in range(ends):
+        out_ref[b] = panel[b * depth : b * depth + depth]
+    lanes = lax.broadcasted_iota(jnp.int32, (depth, width), 1) % n_sub
+    for h in range(1, high):
+        shape = (ends * depth, width)
+        goal = lax.broadcasted_iota(jnp.int32, shape, 0)
+        lane = lax.broadcasted_iota(jnp.int32, shape, 1)
+        b, inner = goal // depth, goal % depth
+        q = (inner // NB * n_col + c) * NB + inner % NB
+        place = (q // (NB * n_row) * NB + q % NB) * n_sub + q // NB % n_row * ends + b
+        pick = (lane == place).astype(f32)
+        chosen = exact_dot(pick, low[:, h * width : h * width + width], (((1,), (1,)), ((), ())))
+        change = exact_dot(chosen, rows_mine)
+        for b in range(ends):
+            value = local_ref[h * ends + b] - change[b * depth : b * depth + depth]
+            out_ref[h * ends + b] = jnp.where(lanes < ends, 0.0, value)
+    for b in range(reach, n_sub):
+        out_ref[b] = jnp.where(lanes < ends, 0.0, local_ref[b])
+
+
+def panel_call(local, gathered, n_row, n_col):
+    n_sub, depth, width = local.shape
+    vectors = depth * n_col
+    whole = pl.BlockSpec(memory_space=pltpu.VMEM)
+    return pl.pallas_call(
+        functools.partial(panel_kernel, n_row, n_col),
+        in_specs=[whole, whole],
+        out_specs=whole,
+        out_shape=jax.ShapeDtypeStruct(local.shape, jnp.float32),
+        scratch_shapes=[pltpu.VMEM((2 * PSUB * vectors, 2 * n_col // (2 * PSUB) * width), jnp.float32)],
+        compiler_params=pltpu.CompilerParams(vmem_limit_bytes=24 * 1024 * 1024),
+    )(local, gathered)
+
+
+def body(own, labels, mobility):
     n_row = lax.axis_size("row")
     n_col = lax.axis_size("col")
+    n_sub = n_row * n_col
+    vectors = own.shape[0]
+    acc, rim, frim, edge, rootx, rooty = gram_call(own, labels, mobility)
 
     def up(values, axis, count):
         return lax.ppermute(values, axis, [(i, i + 1) for i in range(count - 1)])
@@ -300,135 +554,13 @@
     tiles = tile_call(
         acc, frim, edge, rootx, rooty,
         up(rim[:, 1], "row", n_row), down(rim[:, 0], "row", n_row),
-        up(edge, "col", n_col), down(edge, "col", n_col),
+        up(edge, "col", n_col), down(edge, "col", n_col), n_col,
     )
-    vectors = own.shape[0]
-    return tiles[:, : SLOTS * vectors].reshape(vectors, SLOTS, vectors).transpose(1, 2, 0)
-
-
-def shift_grid(values, offset):
-    widths = [(1, 1), (1, 1)] + [(0, 0)] * (values.ndim - 2)
-    padded = jnp.pad(values, widths)
-    start_x = 1 - offset[0]
-    start_y = 1 - offset[1]
-    return padded[start_x : start_x + values.shape[0], start_y : start_y + values.shape[1]]
-
-
-def to_owner(stack, n_row, n_col):
-    slots = stack.shape[0]
-    vectors = stack.shape[1]
-    row_blocks = vectors // (NB * n_row)
-    col_blocks = vectors // (NB * n_col)
-    split = stack.reshape(slots, row_blocks, n_row, NB, col_blocks, n_col, NB)
-    moved = split.transpose(2, 5, 0, 4, 6, 1, 3)
-    return moved.reshape(n_row, n_col, slots * col_blocks * NB * row_blocks * NB)
-
-
-def place_bands(bands, n_row, n_col):
-    n_sub = n_row * n_col
-    sub_x = jnp.arange(n_sub, dtype=jnp.int32) // n_col
-    sub_y = jnp.arange(n_sub, dtype=jnp.int32) % n_col
-    total = None
-    for index in range(9):
-        step_x = index // 3 - 1
-        step_y = index % 3 - 1
-        match = (
-            (sub_x[:, None] == sub_x[None, :] + step_x)
-            & (sub_y[:, None] == sub_y[None, :] + step_y)
-        ).astype(jnp.float32)
-        flat = bands[index].reshape(n_sub, -1).T
-        term = match[:, None, :] * flat[None, :, :]
-        total = term if total is None else total + term
-    return total
-
-
-def body(geneo_vectors, phase_labels, phase_mobility):
-    vectors = geneo_vectors.shape[0]
-    n_row = lax.axis_size("row")
-    n_col = lax.axis_size("col")
-    n_sub = n_row * n_col
-    row_blocks = vectors // (NB * n_row)
-    col_blocks = vectors // (NB * n_col)
-    rows_here = row_blocks * NB * n_sub
-    piece_len = col_blocks * NB * row_blocks * NB
-    width = PSUB * vectors
-    tiles = local_tiles(geneo_vectors, phase_labels, phase_mobility)
-    offsets = slot_offsets()
-    routed = lax.all_to_all(
-        lax.all_to_all(
-            to_owner(tiles, n_row, n_col), "row", split_axis=0, concat_axis=0, tiled=True
-        ),
-        "col",
-        split_axis=1,
-        concat_axis=1,
-        tiled=True,
+    local, gathered = trade_call(tiles, n_row, n_col)
+    local = panel_call(local, gathered, n_row, n_col)
+    return local.reshape(
+        n_sub, vectors // (NB * n_col), 1, NB, vectors // (NB * n_row), 1, NB, n_sub
     )
-    routed = routed.reshape(n_row, n_col, len(offsets), piece_len)
-    bands = [jnp.zeros((n_row, n_col, piece_len), jnp.float32) for count in range(9)]
-    for slot, pair_off in enumerate(offsets):
-        place = band_index(pair_off[0], pair_off[1])
-        bands[place] = bands[place] + shift_grid(routed[:, :, slot], pair_off[0])
-    local = place_bands(bands, n_row, n_col).reshape(n_sub, col_blocks * NB, rows_here)
-    row_index = lax.axis_index("row")
-    col_index = lax.axis_index("col")
-    row_sub = jnp.arange(rows_here, dtype=jnp.int32) % n_sub
-    ends = 2 * PSUB
-    mine = local[:ends].reshape(ends, col_blocks, NB, rows_here)
-    parts = lax.all_gather(mine, ("row", "col"), axis=0, tiled=False)
-    parts = parts.reshape(n_row, n_col, ends, col_blocks, NB, rows_here)
-    panels = parts.transpose(2, 3, 1, 4, 0, 5).reshape(2, width, n_row, rows_here)
-
-    def rows_of(block, first, last):
-        grid = block.reshape(width, n_row, row_blocks, NB, n_sub)[..., first:last]
-        return grid.transpose(0, 4, 2, 1, 3).reshape(width, (last - first) * vectors)
-
-    done = []
-    for panel in range(2):
-        first = panel * PSUB
-        last = first + PSUB
-        block = panels[panel]
-        for solved in done:
-            change = lax.dot_general(
-                rows_of(solved, first, last),
-                solved.reshape(width, n_row * rows_here),
-                (((0,), (0,)), ((), ())),
-                precision=lax.Precision.HIGHEST,
-                preferred_element_type=jnp.float32,
-            )
-            block = block - change.reshape(width, n_row, rows_here)
-        block = jnp.where(row_sub >= first, block, jnp.float32(0.0))
-        low = jnp.linalg.cholesky(rows_of(block, first, last).T)
-        solved = lax.linalg.triangular_solve(
-            low, block.reshape(width, n_row * rows_here), left_side=True, lower=True
-        ).reshape(width, n_row, rows_here)
-        done.append(solved)
-    both = jnp.concatenate(done, axis=0)
-    rows_mine = lax.dynamic_index_in_dim(both, row_index, 1, keepdims=False)
-    by_block = both.reshape(2 * width, n_row, row_blocks, NB, n_sub).transpose(0, 2, 1, 3, 4)
-    picked = lax.dynamic_index_in_dim(
-        by_block.reshape(2 * width, row_blocks, n_row // n_col, n_col, NB, n_sub),
-        col_index,
-        3,
-        keepdims=False,
-    )
-    columns = (
-        picked.reshape(2 * width, col_blocks * NB, n_sub)
-        .transpose(0, 2, 1)
-        .reshape(2 * width, n_sub * col_blocks * NB)
-    )
-    update = lax.dot_general(
-        columns,
-        rows_mine,
-        (((0,), (0,)), ((), ())),
-        precision=lax.Precision.HIGHEST,
-        preferred_element_type=jnp.float32,
-    ).reshape(n_sub, col_blocks * NB, rows_here)
-    panel_mine = lax.dynamic_index_in_dim(
-        rows_mine.reshape(ends, col_blocks, n_col, NB, rows_here), col_index, 2, keepdims=False
-    ).reshape(ends, col_blocks * NB, rows_here)
-    rest = jnp.where(row_sub < ends, jnp.float32(0.0), local[ends:] - update[ends:])
-    local = jnp.concatenate([panel_mine, rest], axis=0)
-    return local.reshape(n_sub, col_blocks, 1, NB, row_blocks, 1, NB, n_sub)
 
 
 def solution(mesh):

time: 177 us -> 111 us (0.63)
  blocking collectives: 38.7 us -> 0 us
  Pallas kernels: 55.8 us -> 85.5 us
  other arithmetic: 26.8 us -> 0 us
  starting transfers between devices: 21.5 us -> 11.2 us
  waiting for transfers between devices: 19.8 us -> 11.2 us
  local copies, waits for them, and re-layouts: 11.7 us -> 3.15 us
    all_gather x1 -> x0, blocking collectives: 38.7 us -> none  [body(): parts = lax.all_gather(mine, ('row', 'col'), axis=0, tiled=False)]
    pallas_call x0 -> x2, Pallas kernels: none -> 29.7 us  [the longest x1 18 us: trade_call(): pl.pallas_call(functools.partial(trade_kernel, n_row, n_col), in_specs=[w...]
    another operation x10 -> x0, other arithmetic: 24.1 us -> none  [the longest x6 13 us: body(): low = jnp.linalg.cholesky(rows_of(block, first, last).T)]
    all_to_all x2 -> x0, starting transfers between devices: 12.3 us -> none  [the longest x1 9 us: body(): lax.all_to_all(to_owner(tiles, n_row, n_col), 'row', split_axis=0, concat...]
    all_to_all x2 -> x0, waiting for transfers between devices: 11.3 us -> none  [the longest x1 7.1 us: body(): lax.all_to_all(to_owner(tiles, n_row, n_col), 'row', split_axis=0, concat...]
    transpose x17 -> x0, local copies, waits for them, and re-layouts: 4.53 us -> none  [the longest x1 2.32 us: to_owner(): moved = split.transpose(2, 5, 0, 4, 6, 1, 3)]
    ppermute x2, waiting for transfers between devices: 3.81 us -> 6.69 us  [up(): return lax.ppermute(values, axis, [(i, i + 1) for i in range(count - 1)])]
    ppermute x2, starting transfers between devices: 6.66 us -> 8.57 us  [up(): return lax.ppermute(values, axis, [(i, i + 1) for i in range(count - 1)])]
  transfers between devices with their start and end apart: 6 -> 4, of which waited for: 4 -> 2; matrix products, arithmetic and copies ran while one was open for 0% -> 0% of each run, Pallas kernels for 0% -> 0%
where the time goes in v2:
time: 111 us
  Pallas kernels  85.5 us (77%)
  starting transfers between devices  11.2 us (10%)
  waiting for transfers between devices  11.2 us (10%)
  local copies, waits for them, and re-layouts  3.15 us (3%)
    pallas_call x1, Pallas kernels, gram_call(): pl.pallas_call(gram_kernel, grid=(n_z + 1,), in_specs=[pl.BlockSpec(memor...  52 us
    pallas_call x1, Pallas kernels, trade_call(): pl.pallas_call(functools.partial(trade_kernel, n_row, n_col), in_specs=[w...  18 us
    pallas_call x1, Pallas kernels, panel_call(): pl.pallas_call(functools.partial(panel_kernel, n_row, n_col), in_specs=[w...  11.7 us
    ppermute x2, starting transfers between devices, up(): return lax.ppermute(values, axis, [(i, i + 1) for i in range(count - 1)])  8.57 us
    ppermute x2, waiting for transfers between devices, up(): return lax.ppermute(values, axis, [(i, i + 1) for i in range(count - 1)])  6.69 us
    ppermute x2, waiting for transfers between devices, down(): return lax.ppermute(values, axis, [(i + 1, i) for i in range(count - 1)])  4.53 us
    pallas_call x1, Pallas kernels, tile_call(): pl.pallas_call(tile_kernel, in_specs=[whole] * 9, out_specs=whole, out_sh...  3.84 us
    ppermute x2, starting transfers between devices, down(): return lax.ppermute(values, axis, [(i + 1, i) for i in range(count - 1)])  2.58 us
  transfers between devices with their start and end apart: 4, of which 2 were waited for; matrix products, arithmetic and copies ran while one was open for 0% of the time, Pallas kernels for 0%

profile of v2, /device:TPU:0, one launch (start us, length us, event | category | flops | bytes accessed | tf_op | source)
XLA Modules:
  0.0 111.1 jit_solution(15798385642316001412)
XLA Ops:
  0.0 0.0 copy-start
  0.0 1.2 %copy-done = s32[32,64,128]{2,1,0:T(8,128)S(1)} copy-done((s32[32,64,128]{2,1,0:T(8,128)S(1)}, s32[32,64,128]{2,1,0:T(8,128)}, u32[]{:S(2)}) %copy-start) | copy-done | bytes 1048600
  1.2 0.0 copy-start.1
  1.2 0.7 copy-done.1
  1.9 52.0 %shard_map.37 = (f32[256,256]{1,0:T(8,128)S(1)}, bf16[32,2,32,128]{3,2,1,0:T(8,128)(2,1)S(1)}, bf16[32,2,32,128]{3,2,1,0:T(8,128)(2,1)S(1)}, bf16[32,64,128]{2,1...) custom-call(f32[4]{0:T(128)S(1)} %copy-done.1, bf16[32,32,64,128]{3,2,1,0:T(8,128)(2,1)} %own_ref.1, ...), custom_call_target="tpu_custom_call" | custom-call | tf_op jit(solution)/shard_map/pallas_call | solution.py:124
  53.9 1.3 %collective-permute-start.3 = (bf16[32,64,128]{2,1,0:T(8,128)(2,1)S(1)}, bf16[32,64,128]{2,1,0:T(8,128)(2,1)S(1)}, u32[]{:S(2)}, u32[]{:S(2)}) collective-permute-start(bf16[32,64,128]{2,1,0:T(8,128)(2,1)S(1)} %get-tuple-element.15.edge_ref), channel_id=1, source_target_pairs={{1,0},{2,1},{3,2},{5,4},{6,5},{7,6},{9,8},{10,9},{11,10},{13,12},{... | collective-permute-start | bytes 1572872 | tf_op jit(solution)/shard_map/ppermute | solution.py:552
  55.2 3.1 %collective-permute-start.2 = (bf16[32,64,128]{2,1,0:T(8,128)(2,1)S(1)}, bf16[32,64,128]{2,1,0:T(8,128)(2,1)S(1)}, u32[]{:S(2)}, u32[]{:S(2)}) collective-permute-start(bf16[32,64,128]{2,1,0:T(8,128)(2,1)S(1)} %get-tuple-element.15.edge_ref), channel_id=1, source_target_pairs={{0,1},{1,2},{2,3},{4,5},{5,6},{6,7},{8,9},{9,10},{10,11},{12,13},{... | collective-permute-start | bytes 1572872 | tf_op jit(solution)/shard_map/ppermute | solution.py:549
  58.3 1.3 %collective-permute-start.1 = (bf16[32,32,128]{2,1,0:T(8,128)(2,1)S(1)}, bf16[32,32,128]{2,1,0:T(8,128)(2,1)S(1)}, u32[]{:S(2)}, u32[]{:S(2)}) collective-permute-start(bf16[32,32,128]{2,1,0:T(8,128)(2,1)S(1)} %get-tuple-element.21), channel_id=1, source_target_pairs={{4,0},{8,4},{12,8},{16,12},{20,16},{24,20},{28,24},{5,1},{9,5},{13... | collective-permute-start | bytes 786440 | tf_op jit(solution)/shard_map/ppermute | solution.py:552
  59.6 5.5 %collective-permute-start = (bf16[32,32,128]{2,1,0:T(8,128)(2,1)S(1)}, bf16[32,32,128]{2,1,0:T(8,128)(2,1)S(1)}, u32[]{:S(2)}, u32[]{:S(2)}) collective-permute-start(bf16[32,32,128]{2,1,0:T(8,128)(2,1)S(1)} %get-tuple-element.22), channel_id=1, source_target_pairs={{0,4},{4,8},{8,12},{12,16},{16,20},{20,24},{24,28},{1,5},{5,9},{9,... | collective-permute-start | bytes 786440 | tf_op jit(solution)/shard_map/ppermute | solution.py:549
  65.1 4.5 %collective-permute-done.1.xupp_ref = bf16[32,32,128]{2,1,0:T(8,128)(2,1)S(1)} collective-permute-done((bf16[32,32,128]{2,1,0:T(8,128)(2,1)S(1)}, bf16[32,32,128]{2,1,0:T(8,128)(2,1)S(1)}, u32[]{:S(2)}, u32[]{:S(2)}) %collective-permute-start.1) | collective-permute-done | bytes 262176 | tf_op jit(solution)/shard_map/ppermute | solution.py:552
  69.6 6.7 %collective-permute-done.xlow_ref = bf16[32,32,128]{2,1,0:T(8,128)(2,1)S(1)} collective-permute-done((bf16[32,32,128]{2,1,0:T(8,128)(2,1)S(1)}, bf16[32,32,128]{2,1,0:T(8,128)(2,1)S(1)}, u32[]{:S(2)}, u32[]{:S(2)}) %collective-permute-start) | collective-permute-done | bytes 262176 | tf_op jit(solution)/shard_map/ppermute | solution.py:549
  76.3 0.0 collective-permute-done.3.yupp_ref
  76.3 0.0 collective-permute-done.2.ylow_ref
  76.3 3.8 %shard_map.38.tile_ref = f32[32,768]{1,0:T(8,128)S(1)} custom-call(f32[256,256]{1,0:T(8,128)S(1)} %get-tuple-element.13.acc_ref, bf16[32,2,32,128]{3,2,1,0:T(8,128)(2,1)S(1)} %get-tuple-element.14.frim_ref, bf16[32,64,128]{2,1,0:T(8,128)(2,1)S(1)} %get-tuple-element.15.edge_ref, f32[32,2,128]{2,1,0:T(2,128)S(1)} %get-tuple-element.16.rootx_ref, ...), custom_call_target="tpu_custom_call" | custom-call | tf_op jit(solution)/shard_map/pallas_call | solution.py:260
  80.2 18.0 %shard_map.39 = (f32[32,8,128]{2,1,0:T(8,128)S(1)}, f32[32,8,128]{2,1,0:T(8,128)S(1)}) custom-call(f32[32,768]{1,0:T(8,128)S(1)} %shard_map.38.tile_ref), custom_call_target="tpu_custom_call" | custom-call | tf_op jit(solution)/shard_map/pallas_call | solution.py:424
  98.2 11.7 %shard_map.40 = f32[32,8,128]{2,1,0:T(8,128)S(1)} custom-call(f32[32,8,128]{2,1,0:T(8,128)S(1)} %get-tuple-element.19.local_ref, f32[32,8,128]{2,1,0:T(8,128)S(1)} %get-tuple-element.20.all_ref), custom_call_target="tpu_custom_call" | custom-call | tf_op jit(solution)/shard_map/pallas_call | solution.py:531
  109.8 1.2 %reshape.3 = f32[32,4,1,2,2,1,2,32]{7,6,4,3,1,0,5,2:T(2,128)} reshape(f32[32,8,128]{2,1,0:T(8,128)S(1)} %shard_map.40) | data formatting | bytes 262144 | tf_op jit(solution)/shard_map/reshape | solution.py:561
  (1 shorter events, 0.0 us)
Async XLA Ops:
  0.0 1.2 %copy-start = (s32[32,64,128]{2,1,0:T(8,128)S(1)}, s32[32,64,128]{2,1,0:T(8,128)}, u32[]{:S(2)}) copy-start(s32[32,64,128]{2,1,0:T(8,128)} %lab_ref.1) | copy-start | bytes 3145732
  1.2 0.7 copy-start.1
  53.9 22.5 %collective-permute-start.3 = (bf16[32,64,128]{2,1,0:T(8,128)(2,1)S(1)}, bf16[32,64,128]{2,1,0:T(8,128)(2,1)S(1)}, u32[]{:S(2)}, u32[]{:S(2)}) collective-permute-start(bf16[32,64,128]{2,1,0:T(8,128)(2,1)S(1)} %get-tuple-element.15.edge_ref), channel_id=1, source_target_pairs={{1,0},{2,1},{3,2},{5,4},{6,5},{7,6},{9,8},{10,9},{11,10},{13,12},{... | collective-permute-start | bytes 1572872 | tf_op jit(solution)/shard_map/ppermute | solution.py:552
  55.2 21.2 %collective-permute-start.2 = (bf16[32,64,128]{2,1,0:T(8,128)(2,1)S(1)}, bf16[32,64,128]{2,1,0:T(8,128)(2,1)S(1)}, u32[]{:S(2)}, u32[]{:S(2)}) collective-permute-start(bf16[32,64,128]{2,1,0:T(8,128)(2,1)S(1)} %get-tuple-element.15.edge_ref), channel_id=1, source_target_pairs={{0,1},{1,2},{2,3},{4,5},{5,6},{6,7},{8,9},{9,10},{10,11},{12,13},{... | collective-permute-start | bytes 1572872 | tf_op jit(solution)/shard_map/ppermute | solution.py:549
  58.3 11.3 %collective-permute-start.1 = (bf16[32,32,128]{2,1,0:T(8,128)(2,1)S(1)}, bf16[32,32,128]{2,1,0:T(8,128)(2,1)S(1)}, u32[]{:S(2)}, u32[]{:S(2)}) collective-permute-start(bf16[32,32,128]{2,1,0:T(8,128)(2,1)S(1)} %get-tuple-element.21), channel_id=1, source_target_pairs={{4,0},{8,4},{12,8},{16,12},{20,16},{24,20},{28,24},{5,1},{9,5},{13... | collective-permute-start | bytes 786440 | tf_op jit(solution)/shard_map/ppermute | solution.py:552
  59.6 16.7 %collective-permute-start = (bf16[32,32,128]{2,1,0:T(8,128)(2,1)S(1)}, bf16[32,32,128]{2,1,0:T(8,128)(2,1)S(1)}, u32[]{:S(2)}, u32[]{:S(2)}) collective-permute-start(bf16[32,32,128]{2,1,0:T(8,128)(2,1)S(1)} %get-tuple-element.22), channel_id=1, source_target_pairs={{0,4},{4,8},{8,12},{12,16},{16,20},{20,24},{24,28},{1,5},{5,9},{9,... | collective-permute-start | bytes 786440 | tf_op jit(solution)/shard_map/ppermute | solution.py:549

commit v3 on v2

v3 whole, which is shorter than its diff:
```python
import functools

import jax
import jax.numpy as jnp
from jax import lax
from jax.experimental import pallas as pl
from jax.experimental.pallas import tpu as pltpu
from jax.sharding import PartitionSpec as P

NB = 2
PSUB = 2
SLOTS = 21
MESH = pl.DeviceIdType.MESH
PLAIN = (((1,), (0,)), ((), ()))


FACES = ((-1, 0), (1, 0), (0, -1), (0, 1))


def slot_offsets():
    offsets = [((0, 0), (0, 0))]
    for face in FACES:
        offsets += [((0, 0), face), (face, (0, 0)), (face, face)]
    for face_x in FACES[:2]:
        for face_y in FACES[2:]:
            offsets += [(face_x, face_y), (face_y, face_x)]
    return offsets


def exact_dot(left, right, dims=PLAIN):
    return lax.dot_general(left, right, dims, precision=lax.Precision.HIGHEST, preferred_element_type=jnp.float32)


def swap_bits(tiles, bits):
    lanes = lax.broadcasted_iota(jnp.int32, tiles[0].shape, 1)
    width = tiles[0].shape[1]
    for index, lane in bits:
        low = lanes // lane % 2 == 0
        out = list(tiles)
        for i in range(len(tiles)):
            if i // index % 2 == 0:
                a, b = tiles[i], tiles[i + index]
                out[i] = jnp.where(low, a, pltpu.roll(b, lane, 1))
                out[i + index] = jnp.where(low, pltpu.roll(a, width - lane, 1), b)
        tiles = out
    return tiles


def powers(count):
    return [1 << i for i in range(count.bit_length() - 1)]


def trade(n_row, n_col, tile_ref, out_ref, all_ref, send_ref, mine_ref, here_ref,
          send_sem, recv_sem, send_sem2, recv_sem2):
    vectors = tile_ref.shape[0]
    n_sub = n_row * n_col
    col_blocks = vectors // (NB * n_col)
    width = n_col * vectors
    depth = col_blocks * NB
    r = lax.axis_index("row")
    c = lax.axis_index("col")
    me = r * n_col + c

    def peer(k):
        other = lax.rem(me + k, n_sub)
        return other, (other // n_col, lax.rem(other, n_col))

    at = lax.broadcasted_iota(jnp.int32, (vectors, vectors), 0)
    source = (at // NB % col_blocks * n_col + at // (NB * col_blocks)) * NB + at % NB
    turn = (source == lax.broadcasted_iota(jnp.int32, (vectors, vectors), 1)).astype(jnp.float32)
    ordered = exact_dot(turn, tile_ref[...])
    packs = tile_ref.shape[1] // width
    blank = jnp.zeros((depth, width), jnp.float32)
    for column in range(n_col):
        some = slice(column * depth, column * depth + depth)
        tiles = [ordered[some, k * width : k * width + width] if k < packs else blank for k in range(n_row)]
        tiles = swap_bits(tiles, [(bit, NB * bit) for bit in powers(n_row)])
        for row in range(n_row):
            send_ref[row * n_col + column] = tiles[row]

    def exchange(kind, source_of, target_ref, sends, recvs):
        def copy(k):
            other, where = peer(k)
            return pltpu.make_async_remote_copy(
                src_ref=source_of(other), dst_ref=target_ref.at[me], send_sem=sends.at[other], recv_sem=recvs.at[me],
                device_id=where, device_id_type=MESH)

        def begin(k, carry):
            copy(k).start()
            return carry

        lax.fori_loop(1, n_sub, begin, 0)

        def finish(k, carry):
            other, where = peer(k)
            pltpu.make_async_remote_copy(
                src_ref=source_of(other), dst_ref=target_ref.at[other], send_sem=sends.at[other],
                recv_sem=recvs.at[other], device_id=where, device_id_type=MESH).wait_recv()
            return carry

        lax.fori_loop(1, n_sub, finish, 0)

        def drain(k, carry):
            copy(k).wait_send()
            return carry

        lax.fori_loop(1, n_sub, drain, 0)

    here_ref[me] = send_ref[me]
    exchange("tiles", lambda other: send_ref.at[other], here_ref, send_sem, recv_sem)

    tiles = [here_ref[s] for s in range(n_sub)]
    quads = n_sub // n_row
    bits = [(bit, NB * bit) for bit in powers(n_row)]
    bits += [(n_row * bit, vectors * bit) for bit in powers(quads)]
    tiles = swap_bits(tiles, bits)
    offsets = slot_offsets()
    stack = jnp.concatenate([tiles[slot % quads * n_row + slot // quads] for slot in range(SLOTS)], axis=0)
    into = lax.broadcasted_iota(jnp.int32, (width, width), 1)
    sub, tru = into % n_sub, into // n_sub
    origin = sub // n_row * vectors + (tru // NB * n_row + sub % n_row) * NB + tru % NB
    order = (origin == lax.broadcasted_iota(jnp.int32, (width, width), 0)).astype(jnp.float32)
    stack = exact_dot(stack, order)
    bands = {}
    for slot, (start, stop) in enumerate(offsets):
        value = stack[slot * depth : slot * depth + depth]
        shift = start[0] * n_col + start[1]
        if shift:
            value = pltpu.roll(value, shift % width, 1)
        step = (stop[0] - start[0]) * n_col + stop[1] - start[1]
        bands[step] = bands[step] + value if step in bands else value
    lanes = lax.broadcasted_iota(jnp.int32, (depth, width), 1) % n_sub
    ends = 2 * PSUB
    reach = 2 * n_col
    packed = jnp.zeros((depth, width), jnp.float32)
    for b in range(n_sub):
        value = jnp.zeros((depth, width), jnp.float32)
        for step, band in bands.items():
            if 0 <= b - step < n_sub:
                value = jnp.where(lanes == b - step, band, value)
        out_ref[b] = value
        if b < ends:
            value = jnp.where(lanes < reach, value, 0.0)
            packed = packed + (pltpu.roll(value, reach * b, 1) if b else value)
    mine_ref[...] = packed
    all_ref[me] = packed
    exchange("panel", lambda other: mine_ref, all_ref, send_sem2, recv_sem2)


def panel_kernel(n_row, n_col, local_ref, all_ref, out_ref, low_ref):
    n_sub, depth, width = local_ref.shape
    vectors = depth * n_col
    ends, reach = 2 * PSUB, 2 * n_col
    f32 = jnp.float32
    r = lax.axis_index("row")
    c = lax.axis_index("col")
    order = ends * vectors
    at = lax.broadcasted_iota(jnp.int32, (vectors, vectors), 1)
    col_blocks = depth // NB
    source = (at // NB % col_blocks * n_col + at // (NB * col_blocks)) * NB + at % NB
    turn = (source == lax.broadcasted_iota(jnp.int32, (vectors, vectors), 0)).astype(f32)
    high = reach // ends
    by_column = []
    for column in range(n_col):
        tiles = [all_ref[row * n_col + column] for row in range(n_row)]
        bits = [(bit, ends * bit) for bit in powers(n_row)]
        by_column.append(swap_bits(tiles, bits))
    halves = []
    for h in range(high):
        parts = []
        for b in range(ends):
            parts.append(exact_dot(turn, jnp.concatenate([by_column[column][b * high + h] for column in range(n_col)], axis=0)))
        halves.append(jnp.concatenate(parts, axis=0))
    tall = 8
    count = order // tall
    work = [[halves[h][t * tall : t * tall + tall] for t in range(count)] for h in range(high)]
    for k in range(order):
        t, s = divmod(k, tall)
        b, q = divmod(k, vectors)
        tr, row, u = q // (NB * n_row), q // NB % n_row, q % NB
        lane = (tr * NB + u) * n_sub + row * ends + b
        rows = [work[h][t][s : s + 1] for h in range(high)]
        pivot = rows[0][:, lane : lane + 1]
        scale = lax.rsqrt(pivot)
        scaled = [x * scale for x in rows]
        for h in range(high):
            low_ref[k : k + 1, h * width : h * width + width] = scaled[h]
        for i in range(t, count):
            weight = work[0][i][:, lane : lane + 1] * scale
            for h in range(high):
                work[h][i] = work[h][i] - weight * scaled[h]
    shape = (order, high * width)
    lane = lax.broadcasted_iota(jnp.int32, shape, 1)
    inner = lane % width
    a = lane // width * ends + inner % ends
    p = (inner // (NB * n_sub) * n_row + inner % n_sub // ends) * NB + inner // n_sub % NB
    keep = a * vectors + p >= lax.broadcasted_iota(jnp.int32, shape, 0)
    low = jnp.where(keep, low_ref[...], 0.0)

    shape = (high * width, width)
    lane = lax.broadcasted_iota(jnp.int32, shape, 0)
    goal = lax.broadcasted_iota(jnp.int32, shape, 1)
    inner = lane % width
    a = lane // width * ends + inner % ends
    mine = (inner % n_sub // ends == r) & (inner // n_sub == goal // n_sub) & (a == goal % n_sub)
    rows_mine = exact_dot(low, mine.astype(f32))
    shape = (ends * depth, order)
    goal = lax.broadcasted_iota(jnp.int32, shape, 0)
    lane = lax.broadcasted_iota(jnp.int32, shape, 1)
    b, inner = goal // depth, goal % depth
    q = (inner // NB * n_col + c) * NB + inner % NB
    pick = (lane == b * vectors + q).astype(f32)
    panel = exact_dot(pick, rows_mine)
    for b in range(ends):
        out_ref[b] = panel[b * depth : b * depth + depth]
    lanes = lax.broadcasted_iota(jnp.int32, (depth, width), 1) % n_sub
    for h in range(1, high):
        shape = (ends * depth, width)
        goal = lax.broadcasted_iota(jnp.int32, shape, 0)
        lane = lax.broadcasted_iota(jnp.int32, shape, 1)
        b, inner = goal // depth, goal % depth
        q = (inner // NB * n_col + c) * NB + inner % NB
        place = (q // (NB * n_row) * NB + q % NB) * n_sub + q // NB % n_row * ends + b
        pick = (lane == place).astype(f32)
        chosen = exact_dot(pick, low[:, h * width : h * width + width], (((1,), (1,)), ((), ())))
        change = exact_dot(chosen, rows_mine)
        for b in range(ends):
            value = local_ref[h * ends + b] - change[b * depth : b * depth + depth]
            out_ref[h * ends + b] = jnp.where(lanes < ends, 0.0, value)
    for b in range(reach, n_sub):
        out_ref[b] = jnp.where(lanes < ends, 0.0, local_ref[b])


def panel_call(local, gathered, n_row, n_col):
    n_sub, depth, width = local.shape
    vectors = depth * n_col
    whole = pl.BlockSpec(memory_space=pltpu.VMEM)
    return pl.pallas_call(
        functools.partial(panel_kernel, n_row, n_col),
        in_specs=[whole, whole],
        out_specs=whole,
        out_shape=jax.ShapeDtypeStruct(local.shape, jnp.float32),
        scratch_shapes=[pltpu.VMEM((2 * PSUB * vectors, 2 * n_col // (2 * PSUB) * width), jnp.float32)],
        compiler_params=pltpu.CompilerParams(vmem_limit_bytes=24 * 1024 * 1024),
    )(local, gathered)


ROWS = 8
GROUP = 8
SPOTS = 4
CHUNK = 4
MINOR = (((1,), (1,)), ((), ()))


def slice_step(g, n_z, fresh, mob_ref, own_ref, lab_ref, acc_ref, rims_ref, frims_ref, side_ref, rootx_ref, rooty_ref,
               plain_ref, part_ref, rows_ref, root_ref, lines_ref):
    vectors, n_x, n_y = part_ref.shape
    blocks = n_x // ROWS
    groups = vectors // GROUP
    per = blocks // groups
    lanes = lax.broadcasted_iota(jnp.int32, (n_x, n_y), 1)
    now = lax.rem(g, 2)
    old = 1 - now

    def gram(slot, j):
        both = rows_ref[slot, j]
        acc_ref[...] += lax.dot_general(both, both, MINOR, preferred_element_type=jnp.float32)

    def trip(j, carry):
        root = root_ref[old]
        spot = pl.multiple_of(j * GROUP * ROWS, GROUP * ROWS)
        line = pl.multiple_of(j * GROUP, GROUP)
        ok = (lanes < SPOTS * g + SPOTS) & (lanes >= SPOTS * g)
        fluxes, olds = [], []
        for i in range(GROUP):
            v = j * GROUP + i
            before = plain_ref[old, v, ROWS : ROWS + n_x]
            total = part_ref[v]
            if fresh:
                own = own_ref[v, 0].astype(jnp.float32)
                plain_ref[now, v, ROWS : ROWS + n_x] = own
                total = total + own
                near = plain_ref[now, v, ROWS + 1 : ROWS + 1 + n_x] + plain_ref[now, v, ROWS - 1 : ROWS - 1 + n_x]
                near = near + jnp.where(lanes == n_y - 1, 0.0, pltpu.roll(own, n_y - 1, 1))
                near = near + jnp.where(lanes == 0, 0.0, pltpu.roll(own, 1, 1))
                near = near + before
                part_ref[v] = near - 6.0 * own
                turned = pltpu.roll(own, SPOTS * g + 2, 1)
                side_ref[v] = jnp.where(ok, turned, side_ref[v])
                lines_ref[0, pl.ds(line + i, 1)] = own[:1]
                lines_ref[1, pl.ds(line + i, 1)] = own[n_x - 1 :]
            flux = total * root
            lines_ref[2, pl.ds(line + i, 1)] = flux[:1]
            lines_ref[3, pl.ds(line + i, 1)] = flux[n_x - 1 :]
            fluxes.append(flux)
            olds.append(before)
            if i % 2:
                for b in range(blocks):
                    part = slice(b * ROWS, b * ROWS + ROWS)
                    where = pl.ds(spot + (i - 1) * ROWS, 2 * ROWS)
                    at = (b % per) * 2 * n_y
                    rows_ref[now, b // per, where, at : at + n_y] = jnp.concatenate(
                        [olds[i - 1][part], olds[i][part]], axis=0).astype(jnp.bfloat16)
                    rows_ref[now, b // per, where, at + n_y : at + 2 * n_y] = jnp.concatenate(
                        [fluxes[i - 1][part], fluxes[i][part]], axis=0).astype(jnp.bfloat16)
        gram(old, j)
        return carry

    lax.fori_loop(0, groups, trip, 0)
    if fresh:
        value = jnp.zeros((n_x, n_y), jnp.float32)
        for phase in range(mob_ref.shape[0]):
            value = value + jnp.where(lab_ref[0] == phase, mob_ref[phase], jnp.float32(0.0))
        root = jnp.sqrt(value)
        root_ref[now] = root
        rootx_ref[g, 0:1] = root[:1]
        rootx_ref[g, 1:2] = root[n_x - 1 :]
        ok = (lanes < SPOTS * g + SPOTS) & (lanes >= SPOTS * g)
        rooty_ref[...] = jnp.where(ok, pltpu.roll(root, SPOTS * g + 2, 1), rooty_ref[...])
        for side in range(2):
            rims_ref[side, g] = lines_ref[side].astype(jnp.bfloat16)
    else:
        for j in range(groups):
            gram(now, j)
    for side in range(2):
        frims_ref[side, jnp.maximum(g - 1, 0)] = lines_ref[2 + side].astype(jnp.bfloat16)


def pack_columns(side_ref, pack_ref):
    vectors, n_x, n_y = side_ref.shape
    quarter = n_x // SPOTS
    spot = lax.broadcasted_iota(jnp.int32, (quarter, n_y), 1) % SPOTS

    def one(v, carry):
        for to, column in enumerate((1, 2)):
            total = jnp.zeros((quarter, n_y), jnp.float32)
            for k in range(SPOTS):
                part = side_ref[v, k * quarter : k * quarter + quarter]
                part = pltpu.roll(part, (k - column) % n_y, 1) if k != column else part
                total = jnp.where(spot == k, part, total)
            pack_ref[to, v] = total.astype(jnp.bfloat16)
        return carry

    lax.fori_loop(0, vectors, one, 0)


def x_tiles(tiles_ref, frims_ref, xhalo_ref, rootx_ref, faces_ref, ends_ref):
    _, n_z, vectors, n_y = frims_ref.shape
    thin = lax.broadcasted_iota(jnp.int32, (vectors, n_y), 1)
    for side in range(2):
        total = jnp.zeros((vectors, n_y), jnp.float32)
        for z in range(n_z):
            over = xhalo_ref[side, z].astype(jnp.float32) * rootx_ref[z, side : side + 1]
            at = slice(z * n_y, z * n_y + n_y)
            faces_ref[side, :vectors, at] = frims_ref[side, z]
            faces_ref[side, vectors:, at] = over.astype(jnp.bfloat16)
            ok = (thin >= SPOTS * z) & (thin < SPOTS * z + SPOTS)
            total = jnp.where(ok, pltpu.roll(over, (SPOTS * z + 2) % n_y, 1), total)
        ends_ref[side] = total.astype(jnp.bfloat16)
        gram = lax.dot_general(faces_ref[side], faces_ref[side], MINOR, preferred_element_type=jnp.float32)
        at = (1 + 3 * side) * vectors
        tiles_ref[:, at : at + vectors] = gram[vectors:, :vectors]
        tiles_ref[:, at + vectors : at + 2 * vectors] = gram[:vectors, vectors:]
        tiles_ref[:, at + 2 * vectors : at + 3 * vectors] = gram[vectors:, vectors:]


def fold(square, vectors):
    order = square.shape[0]
    line = lax.broadcasted_iota(jnp.int32, (order, order), 0)
    column = lax.broadcasted_iota(jnp.int32, (order, order), 1)
    pick = (lax.broadcasted_iota(jnp.int32, (order, vectors), 0) // ROWS
            == lax.broadcasted_iota(jnp.int32, (order, vectors), 1)).astype(jnp.float32)
    thick = jnp.where(line % ROWS == column % ROWS, square, 0.0).reshape(vectors, ROWS, order).sum(1)
    return exact_dot(thick, pick)


def y_tiles(tiles_ref, side_ref, rooty_ref, yhalo_ref, ends_ref, left_ref, right_ref, cut_ref):
    vectors, n_x, n_y = side_ref.shape
    order = vectors * ROWS
    blocks = n_x // ROWS
    f32, bf16 = jnp.float32, jnp.bfloat16
    rows = lax.broadcasted_iota(jnp.int32, (n_x, n_y), 0)
    lanes = lax.broadcasted_iota(jnp.int32, (n_x, n_y), 1)
    spot = lanes % SPOTS
    root = jnp.where((spot == 1) | (spot == 2), rooty_ref[...], 0.0)

    def spread(packed, column):
        return jnp.concatenate(
            [pltpu.roll(packed, (column - k) % n_y, 1) if k != column else packed for k in range(SPOTS)], axis=0)

    def pair_of(m, carry):
        kept = []
        for i in range(2):
            v = 2 * m + i
            own = side_ref[v]
            near = jnp.where(lanes < SPOTS, 0.0, pltpu.roll(own, SPOTS, 1))
            near = near + jnp.where(lanes >= n_y - SPOTS, 0.0, pltpu.roll(own, n_y - SPOTS, 1))
            near = near + jnp.where(rows == 0, 0.0, pltpu.roll(own, 1, 0))
            near = near + jnp.where(rows == n_x - 1, 0.0, pltpu.roll(own, n_x - 1, 0))
            near = near + jnp.where(spot == 2, pltpu.roll(own, n_y - 1, 1), pltpu.roll(own, 1, 1))
            flux = (near - 6.0 * own) * root
            low = spread(yhalo_ref[0, v].astype(f32), 2)
            upp = spread(yhalo_ref[1, v].astype(f32), 1)
            over = jnp.where(spot == 2, low, upp) * root
            cut_ref[0, pl.ds(v, 1)] = over[:1]
            cut_ref[1, pl.ds(v, 1)] = over[n_x - 1 :]
            kept.append((flux, over, jnp.where(spot == 2, over, 0.0), jnp.where(spot == 1, over, 0.0)))
        for b in range(blocks):
            part = slice(b * ROWS, b * ROWS + ROWS)
            both = [jnp.concatenate([x[part], y[part]], axis=0).astype(bf16) for x, y in zip(*kept)]
            at = slice(b * n_y, b * n_y + n_y)
            first = pl.ds(pl.multiple_of(m * 2 * ROWS, 2 * ROWS), 2 * ROWS)
            second = pl.ds(pl.multiple_of(order + m * 2 * ROWS, 2 * ROWS), 2 * ROWS)
            left_ref[first, at] = both[0]
            left_ref[second, at] = both[1]
            right_ref[first, at] = both[2]
            right_ref[second, at] = both[3]
        return carry

    lax.fori_loop(0, vectors // 2, pair_of, 0)
    crossed = lax.dot_general(left_ref[...], right_ref[...], MINOR, preferred_element_type=f32)

    def put(slot, value):
        tiles_ref[:, slot * vectors : (slot + 1) * vectors] = value

    for side in range(2):
        here = slice(side * order, side * order + order)
        cross = fold(crossed[:order, here], vectors)
        put(7 + 3 * side, cross.T)
        put(8 + 3 * side, cross)
        put(9 + 3 * side, fold(crossed[order:, here], vectors))
    thin = lax.broadcasted_iota(jnp.int32, (vectors, n_y), 1)
    slot = 13
    for x in range(2):
        for y in range(2):
            along = jnp.where(thin % SPOTS == 2 - y, cut_ref[x], 0.0).astype(bf16)
            put(slot, lax.dot_general(along, ends_ref[x], MINOR, preferred_element_type=f32))
            put(slot + 1, lax.dot_general(ends_ref[x], along, MINOR, preferred_element_type=f32))
            slot += 2


def main_kernel(n_row, n_col, mob_ref, own_ref, lab_ref, out_ref, all_ref,
                plain_ref, part_ref, rows_ref, root_ref, lines_ref, acc_ref, rims_ref, frims_ref, side_ref,
                rootx_ref, rooty_ref, xhalo_ref, pack_ref, yhalo_ref, faces_ref, ends_ref, left_ref, right_ref, cut_ref,
                tiles_ref, message_ref, here_ref, mine_ref, panel_ref,
                xsend_sem, xrecv_sem, ysend_sem, yrecv_sem, send_sem, recv_sem, send_sem2, recv_sem2):
    g = pl.program_id(0)
    n_z = pl.num_programs(0) - 1
    vectors = part_ref.shape[0]
    n_sub = n_row * n_col
    r = lax.axis_index("row")
    c = lax.axis_index("col")
    me = r * n_col + c
    barrier = pltpu.get_barrier_semaphore()

    def peer(k):
        other = lax.rem(me + k, n_sub)
        return other, (other // n_col, lax.rem(other, n_col))

    def rim_copy(side, some):
        return pltpu.make_async_remote_copy(
            src_ref=rims_ref.at[side, some], dst_ref=xhalo_ref.at[1 - side, some],
            send_sem=xsend_sem.at[side], recv_sem=xrecv_sem.at[1 - side],
            device_id=(lax.rem(r + 2 * side - 1 + n_row, n_row), c), device_id_type=MESH)

    def column_copy(way):
        return pltpu.make_async_remote_copy(
            src_ref=pack_ref.at[way], dst_ref=yhalo_ref.at[way],
            send_sem=ysend_sem.at[way], recv_sem=yrecv_sem.at[way],
            device_id=(r, lax.rem(c + 1 - 2 * way + n_col, n_col)), device_id_type=MESH)

    x_there = (r > 0, r < n_row - 1)
    y_there = (c > 0, c < n_col - 1)

    @pl.when(g == 0)
    def _():
        def greet(k, carry):
            pl.semaphore_signal(barrier, inc=1, device_id=peer(k)[1], device_id_type=MESH)
            return carry

        lax.fori_loop(1, n_sub, greet, 0)
        for ref in (plain_ref, part_ref, rows_ref, root_ref, acc_ref, side_ref, rooty_ref):
            ref[...] = jnp.zeros_like(ref)
        tiles_ref[:, SLOTS * vectors :] = jnp.zeros((vectors, tiles_ref.shape[1] - SLOTS * vectors), jnp.float32)
        for side in range(2):
            @pl.when(jnp.logical_not(x_there[side]))
            def _():
                xhalo_ref[side] = jnp.zeros(xhalo_ref.shape[1:], jnp.bfloat16)

            @pl.when(jnp.logical_not(y_there[side]))
            def _():
                yhalo_ref[side] = jnp.zeros(yhalo_ref.shape[1:], jnp.bfloat16)

    @pl.when(g == CHUNK)
    def _():
        pl.semaphore_wait(barrier, n_sub - 1)

    @pl.when((lax.rem(g, CHUNK) == 0) & (g > 0))
    def _():
        for side in range(2):
            @pl.when(x_there[side])
            def _():
                rim_copy(side, pl.ds(g - CHUNK, CHUNK)).start()

    refs = (mob_ref, own_ref, lab_ref, acc_ref, rims_ref, frims_ref, side_ref, rootx_ref, rooty_ref,
            plain_ref, part_ref, rows_ref, root_ref, lines_ref)

    @pl.when(g < n_z)
    def _():
        slice_step(g, n_z, True, *refs)

    @pl.when(g == n_z)
    def _():
        pack_columns(side_ref, pack_ref)
        for way in range(2):
            @pl.when(y_there[1 - way])
            def _():
                column_copy(way).start()
        slice_step(g, n_z, False, *refs)
        tiles_ref[:, :vectors] = fold(acc_ref[...], vectors)
        everything = pl.ds(0, n_z)
        for side in range(2):
            @pl.when(x_there[side])
            def _():
                rim_copy(1 - side, everything).wait_recv()
        x_tiles(tiles_ref, frims_ref, xhalo_ref, rootx_ref, faces_ref, ends_ref)
        for way in range(2):
            @pl.when(y_there[way])
            def _():
                column_copy(way).wait_recv()
        y_tiles(tiles_ref, side_ref, rooty_ref, yhalo_ref, ends_ref, left_ref, right_ref, cut_ref)
        trade(n_row, n_col, tiles_ref, out_ref, panel_ref, message_ref, mine_ref, here_ref,
              send_sem, recv_sem, send_sem2, recv_sem2)
        all_ref[...] = panel_ref[...]
        for side in range(2):
            @pl.when(x_there[side])
            def _():
                rim_copy(side, everything).wait_send()
        for way in range(2):
            @pl.when(y_there[1 - way])
            def _():
                column_copy(way).wait_send()


def main_call(own, labels, mobility, n_row, n_col):
    vectors, n_z, n_x, n_y = own.shape
    n_sub = n_row * n_col
    depth = vectors // n_col
    width = vectors // n_row * n_sub
    order = vectors * ROWS
    blocks = n_x // ROWS
    groups = vectors // GROUP
    f32, bf16 = jnp.float32, jnp.bfloat16
    last = n_z - 1
    pieces = jax.ShapeDtypeStruct((n_sub, depth, width), f32)
    return pl.pallas_call(
        functools.partial(main_kernel, n_row, n_col),
        grid=(n_z + 1,),
        in_specs=[
            pl.BlockSpec(memory_space=pltpu.SMEM),
            pl.BlockSpec((vectors, 1, n_x, n_y), lambda g: (0, jnp.minimum(g, last), 0, 0)),
            pl.BlockSpec((1, n_x, n_y), lambda g: (jnp.minimum(g, last), 0, 0)),
        ],
        out_specs=[pl.BlockSpec((n_sub, depth, width), lambda g: (0, 0, 0))] * 2,
        out_shape=[pieces, pieces],
        scratch_shapes=[
            pltpu.VMEM((2, vectors, n_x + 2 * ROWS, n_y), f32),
            pltpu.VMEM((vectors, n_x, n_y), f32),
            pltpu.VMEM((2, groups, order, blocks // groups * 2 * n_y), bf16),
            pltpu.VMEM((2, n_x, n_y), f32),
            pltpu.VMEM((4, vectors, n_y), f32),
            pltpu.VMEM((order, order), f32),
            pltpu.VMEM((2, n_z, vectors, n_y), bf16),
            pltpu.VMEM((2, n_z, vectors, n_y), bf16),
            pltpu.VMEM((vectors, n_x, n_y), f32),
            pltpu.VMEM((n_z, 2, n_y), f32),
            pltpu.VMEM((n_x, n_y), f32),
            pltpu.VMEM((2, n_z, vectors, n_y), bf16),
            pltpu.VMEM((2, vectors, n_x // SPOTS, n_y), bf16),
            pltpu.VMEM((2, vectors, n_x // SPOTS, n_y), bf16),
            pltpu.VMEM((2, 2 * vectors, n_z * n_y), bf16),
            pltpu.VMEM((2, vectors, n_y), bf16),
            pltpu.VMEM((2 * order, blocks * n_y), bf16),
            pltpu.VMEM((2 * order, blocks * n_y), bf16),
            pltpu.VMEM((2, vectors, n_y), f32),
            pltpu.VMEM((vectors, -(-SLOTS // n_col) * n_col * vectors), f32),
            pltpu.VMEM((n_sub, depth, width), f32),
            pltpu.VMEM((n_sub, depth, width), f32),
            pltpu.VMEM((depth, width), f32),
            pltpu.VMEM((n_sub, depth, width), f32),
            pltpu.SemaphoreType.DMA((2,)),
            pltpu.SemaphoreType.DMA((2,)),
            pltpu.SemaphoreType.DMA((2,)),
            pltpu.SemaphoreType.DMA((2,)),
            pltpu.SemaphoreType.DMA((n_sub,)),
            pltpu.SemaphoreType.DMA((n_sub,)),
            pltpu.SemaphoreType.DMA((n_sub,)),
            pltpu.SemaphoreType.DMA((n_sub,)),
        ],
        compiler_params=pltpu.CompilerParams(
            collective_id=0, has_side_effects=True, vmem_limit_bytes=48 * 1024 * 1024),
    )(mobility, own, labels)


def body(own, labels, mobility):
    n_row = lax.axis_size("row")
    n_col = lax.axis_size("col")
    n_sub = n_row * n_col
    vectors = own.shape[0]
    local, gathered = main_call(own, labels, mobility, n_row, n_col)
    local = panel_call(local, gathered, n_row, n_col)
    return local.reshape(
        n_sub, vectors // (NB * n_col), 1, NB, vectors // (NB * n_row), 1, NB, n_sub
    )


def solution(mesh):
    return jax.shard_map(
        body,
        mesh=mesh,
        in_specs=(P(None, None, "row", "col"), P(None, "row", "col"), P()),
        out_specs=P(None, None, "col", None, None, "row", None, None),
        check_vma=False,
    )
```

time: 111 us -> 94 us (0.85)
  starting transfers between devices: 11.2 us -> 0 us
  waiting for transfers between devices: 11.2 us -> 0 us
  Pallas kernels: 85.5 us -> 90.6 us
    ppermute x4 -> x0, waiting for transfers between devices: 11.2 us -> none  [the longest x2 6.69 us: up(): return lax.ppermute(values, axis, [(i, i + 1) for i in range(count - 1)])]
    ppermute x4 -> x0, starting transfers between devices: 11.2 us -> none  [the longest x2 8.57 us: up(): return lax.ppermute(values, axis, [(i, i + 1) for i in range(count - 1)])]
    pallas_call x3 -> x1, Pallas kernels: 73.8 us -> 79 us  [main_call(): pl.pallas_call(functools.partial(main_kernel, n_row, n_col), grid=(n_z +...]
  transfers between devices with their start and end apart: 4 -> 0, of which waited for: 2 -> 0; matrix products, arithmetic and copies ran while one was open for 0% -> 0% of each run, Pallas kernels for 0% -> 0%
where the time goes in v3:
time: 94 us; the launch traced here: 93.8 us
  Pallas kernels  90.6 us (96%)
  local copies, waits for them, and re-layouts  3.12 us (3%)
    pallas_call x1, Pallas kernels, main_call(): pl.pallas_call(functools.partial(main_kernel, n_row, n_col), grid=(n_z +...  79 us
    pallas_call x1, Pallas kernels, panel_call(): pl.pallas_call(functools.partial(panel_kernel, n_row, n_col), in_specs=[w...  11.7 us

profile of v3, /device:TPU:0, one launch (start us, length us, event | category | flops | bytes accessed | tf_op | source)
XLA Modules:
  0.0 93.8 jit_solution(6450137604504710325)
XLA Ops:
  0.0 0.0 copy-start
  0.0 1.2 %copy-done = s32[32,64,128]{2,1,0:T(8,128)S(1)} copy-done((s32[32,64,128]{2,1,0:T(8,128)S(1)}, s32[32,64,128]{2,1,0:T(8,128)}, u32[]{:S(2)}) %copy-start) | copy-done | bytes 1048600
  1.2 0.0 copy-start.1
  1.2 0.7 copy-done.1
  1.9 79.0 %shard_map.37 = (f32[32,8,128]{2,1,0:T(8,128)S(1)}, f32[32,8,128]{2,1,0:T(8,128)S(1)}) custom-call(f32[4]{0:T(128)S(1)} %copy-done.1, bf16[32,32,64,128]{3,2,1,0:T(8,128)(2,1)} %own_ref.1, s32[32,64,128]{2,1,0:T(8,128)S(1)} %copy-done), custom_call_target="tpu_custom_call" | custom-call | tf_op jit(solution)/shard_map/pallas_call | solution.py:556
  80.8 11.7 %shard_map.38 = f32[32,8,128]{2,1,0:T(8,128)S(1)} custom-call(f32[32,8,128]{2,1,0:T(8,128)S(1)} %get-tuple-element.7.local_ref, f32[32,8,128]{2,1,0:T(8,128)S(1)} %get-tuple-element.8.all_ref), custom_call_target="tpu_custom_call" | custom-call | tf_op jit(solution)/shard_map/pallas_call | solution.py:238
  92.5 1.2 %reshape.3 = f32[32,4,1,2,2,1,2,32]{7,6,4,3,1,0,5,2:T(2,128)} reshape(f32[32,8,128]{2,1,0:T(8,128)S(1)} %shard_map.38) | data formatting | bytes 262144 | tf_op jit(solution)/shard_map/reshape | solution.py:612
Async XLA Ops:
  0.0 1.2 %copy-start = (s32[32,64,128]{2,1,0:T(8,128)S(1)}, s32[32,64,128]{2,1,0:T(8,128)}, u32[]{:S(2)}) copy-start(s32[32,64,128]{2,1,0:T(8,128)} %lab_ref.1) | copy-start | bytes 3145732
  1.2 0.7 copy-start.1

commit v4 on v3

--- a/solution.py
+++ b/solution.py
@@ -246,84 +246,90 @@
 
 
 ROWS = 8
-GROUP = 8
 SPOTS = 4
 CHUNK = 4
 MINOR = (((1,), (1,)), ((), ()))
 
 
-def slice_step(g, n_z, fresh, mob_ref, own_ref, lab_ref, acc_ref, rims_ref, frims_ref, side_ref, rootx_ref, rooty_ref,
-               plain_ref, part_ref, rows_ref, root_ref, lines_ref):
-    vectors, n_x, n_y = part_ref.shape
+def cross_weights(n_y):
+    shape = (2 * n_y, 2 * n_y)
+    i = lax.broadcasted_iota(jnp.int32, shape, 0)
+    j = lax.broadcasted_iota(jnp.int32, shape, 1)
+    gap = i % n_y - j % n_y
+    same = i // n_y == j // n_y
+    near = jnp.where((gap == 1) | (gap == -1), 1.0, jnp.where(gap == 0, -6.0, 0.0))
+    return jnp.where(same, near, jnp.where(gap == 0, 1.0, 0.0)).astype(jnp.bfloat16)
+
+
+def stencil(p, fresh, own_ref, cross_ref, mixed_ref, first_ref, now_ref, old_ref, part_ref, rows_ref, root_ref, side_ref,
+            lines_ref):
+    vectors, n_x, n_y = side_ref.shape
     blocks = n_x // ROWS
-    groups = vectors // GROUP
-    per = blocks // groups
-    lanes = lax.broadcasted_iota(jnp.int32, (n_x, n_y), 1)
-    now = lax.rem(g, 2)
-    old = 1 - now
-
-    def gram(slot, j):
-        both = rows_ref[slot, j]
-        acc_ref[...] += lax.dot_general(both, both, MINOR, preferred_element_type=jnp.float32)
-
-    def trip(j, carry):
-        root = root_ref[old]
-        spot = pl.multiple_of(j * GROUP * ROWS, GROUP * ROWS)
-        line = pl.multiple_of(j * GROUP, GROUP)
-        ok = (lanes < SPOTS * g + SPOTS) & (lanes >= SPOTS * g)
-        fluxes, olds = [], []
-        for i in range(GROUP):
-            v = j * GROUP + i
-            before = plain_ref[old, v, ROWS : ROWS + n_x]
+    inner = slice(ROWS, ROWS + n_x)
+    up, down = slice(ROWS + 1, ROWS + 1 + n_x), slice(ROWS - 1, ROWS - 1 + n_x)
+    if fresh:
+        both = jnp.concatenate([own_ref[:, s].reshape(vectors * n_x, n_y) for s in range(2)], axis=1)
+        mixed_ref[...] = lax.dot_general(both, cross_ref[...], PLAIN, preferred_element_type=jnp.float32)
+        lanes = lax.broadcasted_iota(jnp.int32, (n_x, n_y), 1)
+        z = 2 * p
+        kept = [(lanes < SPOTS * (z + s + 1)) & (lanes >= SPOTS * (z + s)) for s in range(2)]
+    for m in range(vectors // 2):
+        mids, fluxes = [[], []], [[], []]
+        for v in (2 * m, 2 * m + 1):
+            last = old_ref[v, inner]
             total = part_ref[v]
+            mids[0].append(last)
             if fresh:
                 own = own_ref[v, 0].astype(jnp.float32)
-                plain_ref[now, v, ROWS : ROWS + n_x] = own
+                first_ref[v, inner] = own
+                next_own = own_ref[v, 1].astype(jnp.float32)
+                now_ref[v, inner] = next_own
                 total = total + own
-                near = plain_ref[now, v, ROWS + 1 : ROWS + 1 + n_x] + plain_ref[now, v, ROWS - 1 : ROWS - 1 + n_x]
-                near = near + jnp.where(lanes == n_y - 1, 0.0, pltpu.roll(own, n_y - 1, 1))
-                near = near + jnp.where(lanes == 0, 0.0, pltpu.roll(own, 1, 1))
-                near = near + before
-                part_ref[v] = near - 6.0 * own
-                turned = pltpu.roll(own, SPOTS * g + 2, 1)
-                side_ref[v] = jnp.where(ok, turned, side_ref[v])
-                lines_ref[0, pl.ds(line + i, 1)] = own[:1]
-                lines_ref[1, pl.ds(line + i, 1)] = own[n_x - 1 :]
-            flux = total * root
-            lines_ref[2, pl.ds(line + i, 1)] = flux[:1]
-            lines_ref[3, pl.ds(line + i, 1)] = flux[n_x - 1 :]
-            fluxes.append(flux)
-            olds.append(before)
-            if i % 2:
-                for b in range(blocks):
-                    part = slice(b * ROWS, b * ROWS + ROWS)
-                    where = pl.ds(spot + (i - 1) * ROWS, 2 * ROWS)
-                    at = (b % per) * 2 * n_y
-                    rows_ref[now, b // per, where, at : at + n_y] = jnp.concatenate(
-                        [olds[i - 1][part], olds[i][part]], axis=0).astype(jnp.bfloat16)
-                    rows_ref[now, b // per, where, at + n_y : at + 2 * n_y] = jnp.concatenate(
-                        [fluxes[i - 1][part], fluxes[i][part]], axis=0).astype(jnp.bfloat16)
-        gram(old, j)
-        return carry
-
-    lax.fori_loop(0, groups, trip, 0)
-    if fresh:
+                mixed = mixed_ref[v * n_x : v * n_x + n_x]
+                near = mixed[:, :n_y] + (first_ref[v, up] + first_ref[v, down]) + last
+                part_ref[v] = mixed[:, n_y:] + (now_ref[v, up] + now_ref[v, down])
+                flux = near * root_ref[1]
+                for s, value in enumerate((own, next_own)):
+                    lines_ref[s, 0, v : v + 1] = value[:1]
+                    lines_ref[s, 1, v : v + 1] = value[n_x - 1 :]
+                    turned = pltpu.roll(own_ref[v, s], lax.rem(SPOTS * (z + s) + 2, n_y), 1)
+                    side_ref[v] = jnp.where(kept[s], turned, side_ref[v])
+                lines_ref[3, 0, v : v + 1] = flux[:1]
+                lines_ref[3, 1, v : v + 1] = flux[n_x - 1 :]
+                mids[1].append(own)
+                fluxes[1].append(flux)
+            flux = total * root_ref[0]
+            lines_ref[2, 0, v : v + 1] = flux[:1]
+            lines_ref[2, 1, v : v + 1] = flux[n_x - 1 :]
+            fluxes[0].append(flux)
+        where = slice(2 * m * ROWS, 2 * m * ROWS + 2 * ROWS)
+        for b in range(blocks):
+            part = slice(b * ROWS, b * ROWS + ROWS)
+            for s in range(2 if fresh else 1):
+                for which, values in enumerate((mids[s], fluxes[s])):
+                    rows_ref[s, b, where, which * n_y : which * n_y + n_y] = jnp.concatenate(
+                        [value[part] for value in values], axis=0).astype(jnp.bfloat16)
+
+
+def gram(acc_ref, rows_ref, slices):
+    both = jnp.concatenate([rows_ref[s, b] for s in slices for b in range(rows_ref.shape[1])], axis=1)
+    acc_ref[...] += lax.dot_general(both, both, MINOR, preferred_element_type=jnp.float32)
+
+
+def roots(p, mob_ref, lab_ref, root_ref, rootx_ref, rooty_ref):
+    _, n_x, n_y = root_ref.shape
+    lanes = lax.broadcasted_iota(jnp.int32, (n_x, n_y), 1)
+    for s in range(2):
+        z = 2 * p + s
         value = jnp.zeros((n_x, n_y), jnp.float32)
         for phase in range(mob_ref.shape[0]):
-            value = value + jnp.where(lab_ref[0] == phase, mob_ref[phase], jnp.float32(0.0))
+            value = value + jnp.where(lab_ref[s] == phase, mob_ref[phase], jnp.float32(0.0))
         root = jnp.sqrt(value)
-        root_ref[now] = root
-        rootx_ref[g, 0:1] = root[:1]
-        rootx_ref[g, 1:2] = root[n_x - 1 :]
-        ok = (lanes < SPOTS * g + SPOTS) & (lanes >= SPOTS * g)
-        rooty_ref[...] = jnp.where(ok, pltpu.roll(root, SPOTS * g + 2, 1), rooty_ref[...])
-        for side in range(2):
-            rims_ref[side, g] = lines_ref[side].astype(jnp.bfloat16)
-    else:
-        for j in range(groups):
-            gram(now, j)
-    for side in range(2):
-        frims_ref[side, jnp.maximum(g - 1, 0)] = lines_ref[2 + side].astype(jnp.bfloat16)
+        root_ref[1 + s] = jnp.where((lanes == 0) | (lanes == n_y - 1), 0.0, root)
+        rootx_ref[z, 0:1] = root[:1]
+        rootx_ref[z, 1:2] = root[n_x - 1 :]
+        ok = (lanes < SPOTS * z + SPOTS) & (lanes >= SPOTS * z)
+        rooty_ref[...] = jnp.where(ok, pltpu.roll(root, lax.rem(SPOTS * z + 2, n_y), 1), rooty_ref[...])
 
 
 def pack_columns(side_ref, pack_ref):
@@ -335,7 +341,7 @@
         for to, column in enumerate((1, 2)):
             total = jnp.zeros((quarter, n_y), jnp.float32)
             for k in range(SPOTS):
-                part = side_ref[v, k * quarter : k * quarter + quarter]
+                part = side_ref[v, k * quarter : k * quarter + quarter].astype(jnp.float32)
                 part = pltpu.roll(part, (k - column) % n_y, 1) if k != column else part
                 total = jnp.where(spot == k, part, total)
             pack_ref[to, v] = total.astype(jnp.bfloat16)
@@ -374,7 +380,7 @@
     return exact_dot(thick, pick)
 
 
-def y_tiles(tiles_ref, side_ref, rooty_ref, yhalo_ref, ends_ref, left_ref, right_ref, cut_ref):
+def y_tiles(tiles_ref, acc_ref, side_ref, rooty_ref, yhalo_ref, ends_ref, left_ref, right_ref, cut_ref):
     vectors, n_x, n_y = side_ref.shape
     order = vectors * ROWS
     blocks = n_x // ROWS
@@ -392,7 +398,7 @@
         kept = []
         for i in range(2):
             v = 2 * m + i
-            own = side_ref[v]
+            own = side_ref[v].astype(f32)
             near = jnp.where(lanes < SPOTS, 0.0, pltpu.roll(own, SPOTS, 1))
             near = near + jnp.where(lanes >= n_y - SPOTS, 0.0, pltpu.roll(own, n_y - SPOTS, 1))
             near = near + jnp.where(rows == 0, 0.0, pltpu.roll(own, 1, 0))
@@ -404,6 +410,8 @@
             over = jnp.where(spot == 2, low, upp) * root
             cut_ref[0, pl.ds(v, 1)] = over[:1]
             cut_ref[1, pl.ds(v, 1)] = over[n_x - 1 :]
+            cut_ref[2, pl.ds(v, 1)] = flux[:1]
+            cut_ref[3, pl.ds(v, 1)] = flux[n_x - 1 :]
             kept.append((flux, over, jnp.where(spot == 2, over, 0.0), jnp.where(spot == 1, over, 0.0)))
         for b in range(blocks):
             part = slice(b * ROWS, b * ROWS + ROWS)
@@ -419,11 +427,18 @@
 
     lax.fori_loop(0, vectors // 2, pair_of, 0)
     crossed = lax.dot_general(left_ref[...], right_ref[...], MINOR, preferred_element_type=f32)
+    edges = left_ref[:order]
+    edges = lax.dot_general(edges, edges, MINOR, preferred_element_type=f32)
 
     def put(slot, value):
         tiles_ref[:, slot * vectors : (slot + 1) * vectors] = value
 
+    put(0, fold(acc_ref[...] + edges, vectors))
     for side in range(2):
+        flux = cut_ref[2 + side].astype(bf16)
+        for slot, left, right in ((1 + 3 * side, ends_ref[side], flux), (2 + 3 * side, flux, ends_ref[side])):
+            here = slice(slot * vectors, (slot + 1) * vectors)
+            tiles_ref[:, here] = tiles_ref[:, here] + lax.dot_general(left, right, MINOR, preferred_element_type=f32)
         here = slice(side * order, side * order + order)
         cross = fold(crossed[:order, here], vectors)
         put(7 + 3 * side, cross.T)
@@ -440,13 +455,14 @@
 
 
 def main_kernel(n_row, n_col, mob_ref, own_ref, lab_ref, out_ref, all_ref,
-                plain_ref, part_ref, rows_ref, root_ref, lines_ref, acc_ref, rims_ref, frims_ref, side_ref,
+                cross_ref, mixed_ref, first_ref, plain0_ref, plain1_ref, part_ref, rows0_ref, rows1_ref, root_ref, lines_ref, acc_ref, rims_ref, frims_ref, side_ref,
                 rootx_ref, rooty_ref, xhalo_ref, pack_ref, yhalo_ref, faces_ref, ends_ref, left_ref, right_ref, cut_ref,
                 tiles_ref, message_ref, here_ref, mine_ref, panel_ref,
                 xsend_sem, xrecv_sem, ysend_sem, yrecv_sem, send_sem, recv_sem, send_sem2, recv_sem2):
-    g = pl.program_id(0)
-    n_z = pl.num_programs(0) - 1
-    vectors = part_ref.shape[0]
+    p = pl.program_id(0)
+    n_z = rims_ref.shape[1]
+    pairs = n_z // 2
+    vectors = side_ref.shape[0]
     n_sub = n_row * n_col
     r = lax.axis_index("row")
     c = lax.axis_index("col")
@@ -472,14 +488,15 @@
     x_there = (r > 0, r < n_row - 1)
     y_there = (c > 0, c < n_col - 1)
 
-    @pl.when(g == 0)
+    @pl.when(p == 0)
     def _():
         def greet(k, carry):
             pl.semaphore_signal(barrier, inc=1, device_id=peer(k)[1], device_id_type=MESH)
             return carry
 
         lax.fori_loop(1, n_sub, greet, 0)
-        for ref in (plain_ref, part_ref, rows_ref, root_ref, acc_ref, side_ref, rooty_ref):
+        cross_ref[...] = cross_weights(side_ref.shape[2])
+        for ref in (first_ref, plain0_ref, plain1_ref, part_ref, rows0_ref, rows1_ref, root_ref, acc_ref, side_ref, rooty_ref):
             ref[...] = jnp.zeros_like(ref)
         tiles_ref[:, SLOTS * vectors :] = jnp.zeros((vectors, tiles_ref.shape[1] - SLOTS * vectors), jnp.float32)
         for side in range(2):
@@ -491,33 +508,51 @@
             def _():
                 yhalo_ref[side] = jnp.zeros(yhalo_ref.shape[1:], jnp.bfloat16)
 
-    @pl.when(g == CHUNK)
+    @pl.when(2 * p == CHUNK)
     def _():
         pl.semaphore_wait(barrier, n_sub - 1)
 
-    @pl.when((lax.rem(g, CHUNK) == 0) & (g > 0))
+    @pl.when((lax.rem(2 * p, CHUNK) == 0) & (p > 0))
     def _():
         for side in range(2):
             @pl.when(x_there[side])
             def _():
-                rim_copy(side, pl.ds(g - CHUNK, CHUNK)).start()
-
-    refs = (mob_ref, own_ref, lab_ref, acc_ref, rims_ref, frims_ref, side_ref, rootx_ref, rooty_ref,
-            plain_ref, part_ref, rows_ref, root_ref, lines_ref)
-
-    @pl.when(g < n_z)
-    def _():
-        slice_step(g, n_z, True, *refs)
-
-    @pl.when(g == n_z)
+                rim_copy(side, pl.ds(2 * p - CHUNK, CHUNK)).start()
+
+    plains, rows = (plain0_ref, plain1_ref), (rows0_ref, rows1_ref)
+
+    def rims(fresh):
+        if fresh:
+            for side in range(2):
+                for s in range(2):
+                    rims_ref[side, 2 * p + s] = lines_ref[s, side].astype(jnp.bfloat16)
+                frims_ref[side, 2 * p] = lines_ref[3, side].astype(jnp.bfloat16)
+        for side in range(2):
+            frims_ref[side, jnp.maximum(2 * p - 1, 1)] = lines_ref[2, side].astype(jnp.bfloat16)
+
+    for odd in range(2):
+        @pl.when((p < pairs) & (lax.rem(p, 2) == odd))
+        def _():
+            roots(p, mob_ref, lab_ref, root_ref, rootx_ref, rooty_ref)
+            gram(acc_ref, rows[1 - odd], (0, 1))
+            stencil(p, True, own_ref, cross_ref, mixed_ref, first_ref, plains[odd], plains[1 - odd], part_ref,
+                    rows[odd], root_ref, side_ref, lines_ref)
+            root_ref[0] = root_ref[2]
+            rims(True)
+
+    @pl.when(p == pairs)
     def _():
         pack_columns(side_ref, pack_ref)
         for way in range(2):
             @pl.when(y_there[1 - way])
             def _():
                 column_copy(way).start()
-        slice_step(g, n_z, False, *refs)
-        tiles_ref[:, :vectors] = fold(acc_ref[...], vectors)
+        odd = pairs % 2
+        stencil(p, False, own_ref, cross_ref, mixed_ref, first_ref, plains[odd], plains[1 - odd], part_ref, rows[odd],
+                root_ref, side_ref, lines_ref)
+        rims(False)
+        gram(acc_ref, rows[1 - odd], (0, 1))
+        gram(acc_ref, rows[odd], (0,))
         everything = pl.ds(0, n_z)
         for side in range(2):
             @pl.when(x_there[side])
@@ -528,7 +563,7 @@
             @pl.when(y_there[way])
             def _():
                 column_copy(way).wait_recv()
-        y_tiles(tiles_ref, side_ref, rooty_ref, yhalo_ref, ends_ref, left_ref, right_ref, cut_ref)
+        y_tiles(tiles_ref, acc_ref, side_ref, rooty_ref, yhalo_ref, ends_ref, left_ref, right_ref, cut_ref)
         trade(n_row, n_col, tiles_ref, out_ref, panel_ref, message_ref, mine_ref, here_ref,
               send_sem, recv_sem, send_sem2, recv_sem2)
         all_ref[...] = panel_ref[...]
@@ -549,30 +584,34 @@
     width = vectors // n_row * n_sub
     order = vectors * ROWS
     blocks = n_x // ROWS
-    groups = vectors // GROUP
     f32, bf16 = jnp.float32, jnp.bfloat16
-    last = n_z - 1
+    last = n_z // 2 - 1
     pieces = jax.ShapeDtypeStruct((n_sub, depth, width), f32)
     return pl.pallas_call(
         functools.partial(main_kernel, n_row, n_col),
-        grid=(n_z + 1,),
+        grid=(n_z // 2 + 1,),
         in_specs=[
             pl.BlockSpec(memory_space=pltpu.SMEM),
-            pl.BlockSpec((vectors, 1, n_x, n_y), lambda g: (0, jnp.minimum(g, last), 0, 0)),
-            pl.BlockSpec((1, n_x, n_y), lambda g: (jnp.minimum(g, last), 0, 0)),
+            pl.BlockSpec((vectors, 2, n_x, n_y), lambda p: (0, jnp.minimum(p, last), 0, 0)),
+            pl.BlockSpec((2, n_x, n_y), lambda p: (jnp.minimum(p, last), 0, 0)),
         ],
         out_specs=[pl.BlockSpec((n_sub, depth, width), lambda g: (0, 0, 0))] * 2,
         out_shape=[pieces, pieces],
         scratch_shapes=[
-            pltpu.VMEM((2, vectors, n_x + 2 * ROWS, n_y), f32),
+            pltpu.VMEM((2 * n_y, 2 * n_y), bf16),
+            pltpu.VMEM((vectors * n_x, 2 * n_y), f32),
+            pltpu.VMEM((vectors, n_x + 2 * ROWS, n_y), f32),
+            pltpu.VMEM((vectors, n_x + 2 * ROWS, n_y), f32),
+            pltpu.VMEM((vectors, n_x + 2 * ROWS, n_y), f32),
             pltpu.VMEM((vectors, n_x, n_y), f32),
-            pltpu.VMEM((2, groups, order, blocks // groups * 2 * n_y), bf16),
-            pltpu.VMEM((2, n_x, n_y), f32),
-            pltpu.VMEM((4, vectors, n_y), f32),
+            pltpu.VMEM((2, blocks, order, 2 * n_y), bf16),
+            pltpu.VMEM((2, blocks, order, 2 * n_y), bf16),
+            pltpu.VMEM((3, n_x, n_y), f32),
+            pltpu.VMEM((4, 2, vectors, n_y), f32),
             pltpu.VMEM((order, order), f32),
             pltpu.VMEM((2, n_z, vectors, n_y), bf16),
             pltpu.VMEM((2, n_z, vectors, n_y), bf16),
-            pltpu.VMEM((vectors, n_x, n_y), f32),
+            pltpu.VMEM((vectors, n_x, n_y), bf16),
             pltpu.VMEM((n_z, 2, n_y), f32),
             pltpu.VMEM((n_x, n_y), f32),
             pltpu.VMEM((2, n_z, vectors, n_y), bf16),
@@ -582,7 +621,7 @@
             pltpu.VMEM((2, vectors, n_y), bf16),
             pltpu.VMEM((2 * order, blocks * n_y), bf16),
             pltpu.VMEM((2 * order, blocks * n_y), bf16),
-            pltpu.VMEM((2, vectors, n_y), f32),
+            pltpu.VMEM((4, vectors, n_y), f32),
             pltpu.VMEM((vectors, -(-SLOTS // n_col) * n_col * vectors), f32),
             pltpu.VMEM((n_sub, depth, width), f32),
             pltpu.VMEM((n_sub, depth, width), f32),

time: 94 us -> 68.7 us (0.73)
  Pallas kernels: 90.6 us -> 65.4 us
    pallas_call x1, Pallas kernels: 79 us -> 53.7 us  [main_call(): pl.pallas_call(functools.partial(main_kernel, n_row, n_col), grid=(n_z //...]
where the time goes in v4:
time: 68.7 us; the launch traced here: 68.5 us
  Pallas kernels  65.4 us (95%)
  local copies, waits for them, and re-layouts  3.12 us (5%)
    pallas_call x1, Pallas kernels, main_call(): pl.pallas_call(functools.partial(main_kernel, n_row, n_col), grid=(n_z //...  53.7 us
    pallas_call x1, Pallas kernels, panel_call(): pl.pallas_call(functools.partial(panel_kernel, n_row, n_col), in_specs=[w...  11.7 us
    unnamed x4, local copies, waits for them, and re-layouts  1.88 us

profile of v4, /device:TPU:0, one launch (start us, length us, event | category | flops | bytes accessed | tf_op | source)
XLA Modules:
  0.0 68.5 jit_solution(10181968149720022987)
XLA Ops:
  0.0 0.0 copy-start
  0.0 1.2 %copy-done = s32[32,64,128]{2,1,0:T(8,128)S(1)} copy-done((s32[32,64,128]{2,1,0:T(8,128)S(1)}, s32[32,64,128]{2,1,0:T(8,128)}, u32[]{:S(2)}) %copy-start) | copy-done | bytes 1048600
  1.2 0.0 copy-start.1
  1.2 0.7 copy-done.1
  1.9 53.7 %shard_map.37 = (f32[32,8,128]{2,1,0:T(8,128)S(1)}, f32[32,8,128]{2,1,0:T(8,128)S(1)}) custom-call(f32[4]{0:T(128)S(1)} %copy-done.1, bf16[32,32,64,128]{3,2,1,0:T(8,128)(2,1)} %own_ref.1, s32[32,64,128]{2,1,0:T(8,128)S(1)} %copy-done), custom_call_target="tpu_custom_call" | custom-call | tf_op jit(solution)/shard_map/pallas_call | solution.py:590
  55.6 11.7 %shard_map.38 = f32[32,8,128]{2,1,0:T(8,128)S(1)} custom-call(f32[32,8,128]{2,1,0:T(8,128)S(1)} %get-tuple-element.7.local_ref, f32[32,8,128]{2,1,0:T(8,128)S(1)} %get-tuple-element.8.all_ref), custom_call_target="tpu_custom_call" | custom-call | tf_op jit(solution)/shard_map/pallas_call | solution.py:238
  67.3 1.2 %reshape.3 = f32[32,4,1,2,2,1,2,32]{7,6,4,3,1,0,5,2:T(2,128)} reshape(f32[32,8,128]{2,1,0:T(8,128)S(1)} %shard_map.38) | data formatting | bytes 262144 | tf_op jit(solution)/shard_map/reshape | solution.py:651
Async XLA Ops:
  0.0 1.2 %copy-start = (s32[32,64,128]{2,1,0:T(8,128)S(1)}, s32[32,64,128]{2,1,0:T(8,128)}, u32[]{:S(2)}) copy-start(s32[32,64,128]{2,1,0:T(8,128)} %lab_ref.1) | copy-start | bytes 3145732
  1.2 0.7 copy-start.1

commit v5 on v4

--- a/solution.py
+++ b/solution.py
@@ -78,7 +78,7 @@
         for row in range(n_row):
             send_ref[row * n_col + column] = tiles[row]
 
-    def exchange(kind, source_of, target_ref, sends, recvs):
+    def exchange(source_of, target_ref, sends, recvs, meanwhile=None):
         def copy(k):
             other, where = peer(k)
             return pltpu.make_async_remote_copy(
@@ -90,6 +90,8 @@
             return carry
 
         lax.fori_loop(1, n_sub, begin, 0)
+        if meanwhile:
+            meanwhile()
 
         def finish(k, carry):
             other, where = peer(k)
@@ -107,7 +109,7 @@
         lax.fori_loop(1, n_sub, drain, 0)
 
     here_ref[me] = send_ref[me]
-    exchange("tiles", lambda other: send_ref.at[other], here_ref, send_sem, recv_sem)
+    exchange(lambda other: send_ref.at[other], here_ref, send_sem, recv_sem)
 
     tiles = [here_ref[s] for s in range(n_sub)]
     quads = n_sub // n_row
@@ -133,21 +135,24 @@
     ends = 2 * PSUB
     reach = 2 * n_col
     packed = jnp.zeros((depth, width), jnp.float32)
-    for b in range(n_sub):
+
+    def place(b):
         value = jnp.zeros((depth, width), jnp.float32)
         for step, band in bands.items():
             if 0 <= b - step < n_sub:
                 value = jnp.where(lanes == b - step, band, value)
         out_ref[b] = value
-        if b < ends:
-            value = jnp.where(lanes < reach, value, 0.0)
-            packed = packed + (pltpu.roll(value, reach * b, 1) if b else value)
+        return value
+
+    for b in range(ends):
+        value = jnp.where(lanes < reach, place(b), 0.0)
+        packed = packed + (pltpu.roll(value, reach * b, 1) if b else value)
     mine_ref[...] = packed
     all_ref[me] = packed
-    exchange("panel", lambda other: mine_ref, all_ref, send_sem2, recv_sem2)
-
-
-def panel_kernel(n_row, n_col, local_ref, all_ref, out_ref, low_ref):
+    exchange(lambda other: mine_ref, all_ref, send_sem2, recv_sem2, lambda: [place(b) for b in range(ends, n_sub)])
+
+
+def panels(n_row, n_col, local_ref, all_ref, out_ref, low_ref):
     n_sub, depth, width = local_ref.shape
     vectors = depth * n_col
     ends, reach = 2 * PSUB, 2 * n_col
@@ -174,21 +179,52 @@
     tall = 8
     count = order // tall
     work = [[halves[h][t * tall : t * tall + tall] for t in range(count)] for h in range(high)]
-    for k in range(order):
-        t, s = divmod(k, tall)
+    def spread(value, s):
+        return jnp.broadcast_to(value[s : s + 1], (tall, width))
+
+    def spot(k):
         b, q = divmod(k, vectors)
         tr, row, u = q // (NB * n_row), q // NB % n_row, q % NB
-        lane = (tr * NB + u) * n_sub + row * ends + b
-        rows = [work[h][t][s : s + 1] for h in range(high)]
-        pivot = rows[0][:, lane : lane + 1]
-        scale = lax.rsqrt(pivot)
-        scaled = [x * scale for x in rows]
-        for h in range(high):
-            low_ref[k : k + 1, h * width : h * width + width] = scaled[h]
-        for i in range(t, count):
-            weight = work[0][i][:, lane : lane + 1] * scale
+        return (tr * NB + u) * n_sub + row * ends + b
+
+    def column(i, k):
+        at = spot(k)
+        return jnp.broadcast_to(work[0][i][:, at : at + 1], (tall, width)) * ones
+
+    ones = jnp.where(all_ref[0] == all_ref[0], 1.0, 0.0)
+    ones = jnp.concatenate([ones] * (tall // depth), axis=0)
+
+    few = 4
+    for first in range(0, order, few):
+        t, base = divmod(first, tall)
+        columns = [column(t, first + s) for s in range(few)]
+        rows = [[spread(work[h][t], base + s) for h in range(high)] for s in range(few)]
+        scaled, weights = [], {}
+        for s in range(few):
+            pivot = spread(columns[s], base + s)
+            inverse = 1.0 / pivot
+            root = lax.rsqrt(pivot)
+            k = first + s
             for h in range(high):
-                work[h][i] = work[h][i] - weight * scaled[h]
+                low_ref[k : k + 1, h * width : h * width + width] = (rows[s][h] * root)[:1]
+            scaled.append([x * inverse for x in rows[s]])
+            for s2 in range(s + 1, few):
+                weight = spread(columns[s], base + s2) * inverse
+                weights[s, s2] = weight
+                rows[s2] = [y - weight * x for x, y in zip(rows[s], rows[s2])]
+                columns[s2] = columns[s2] - weight * columns[s]
+        done = base + few == tall
+        for i in range(t + done, count):
+            if i > t:
+                columns = [column(i, first + s) for s in range(few)]
+                for s in range(few):
+                    for s2 in range(s + 1, few):
+                        columns[s2] = columns[s2] - weights[s, s2] * columns[s]
+            for h in range(high):
+                total = columns[0] * scaled[0][h]
+                for s in range(1, few):
+                    total = total + columns[s] * scaled[s][h]
+                work[h][i] = work[h][i] - total
     shape = (order, high * width)
     lane = lax.broadcasted_iota(jnp.int32, shape, 1)
     inner = lane % width
@@ -229,20 +265,6 @@
             out_ref[h * ends + b] = jnp.where(lanes < ends, 0.0, value)
     for b in range(reach, n_sub):
         out_ref[b] = jnp.where(lanes < ends, 0.0, local_ref[b])
-
-
-def panel_call(local, gathered, n_row, n_col):
-    n_sub, depth, width = local.shape
-    vectors = depth * n_col
-    whole = pl.BlockSpec(memory_space=pltpu.VMEM)
-    return pl.pallas_call(
-        functools.partial(panel_kernel, n_row, n_col),
-        in_specs=[whole, whole],
-        out_specs=whole,
-        out_shape=jax.ShapeDtypeStruct(local.shape, jnp.float32),
-        scratch_shapes=[pltpu.VMEM((2 * PSUB * vectors, 2 * n_col // (2 * PSUB) * width), jnp.float32)],
-        compiler_params=pltpu.CompilerParams(vmem_limit_bytes=24 * 1024 * 1024),
-    )(local, gathered)
 
 
 ROWS = 8
@@ -454,10 +476,10 @@
             slot += 2
 
 
-def main_kernel(n_row, n_col, mob_ref, own_ref, lab_ref, out_ref, all_ref,
+def main_kernel(n_row, n_col, mob_ref, own_ref, lab_ref, out_ref,
                 cross_ref, mixed_ref, first_ref, plain0_ref, plain1_ref, part_ref, rows0_ref, rows1_ref, root_ref, lines_ref, acc_ref, rims_ref, frims_ref, side_ref,
                 rootx_ref, rooty_ref, xhalo_ref, pack_ref, yhalo_ref, faces_ref, ends_ref, left_ref, right_ref, cut_ref,
-                tiles_ref, message_ref, here_ref, mine_ref, panel_ref,
+                tiles_ref, message_ref, here_ref, mine_ref, panel_ref, local_ref, low_ref,
                 xsend_sem, xrecv_sem, ysend_sem, yrecv_sem, send_sem, recv_sem, send_sem2, recv_sem2):
     p = pl.program_id(0)
     n_z = rims_ref.shape[1]
@@ -564,9 +586,9 @@
             def _():
                 column_copy(way).wait_recv()
         y_tiles(tiles_ref, acc_ref, side_ref, rooty_ref, yhalo_ref, ends_ref, left_ref, right_ref, cut_ref)
-        trade(n_row, n_col, tiles_ref, out_ref, panel_ref, message_ref, mine_ref, here_ref,
+        trade(n_row, n_col, tiles_ref, local_ref, panel_ref, message_ref, mine_ref, here_ref,
               send_sem, recv_sem, send_sem2, recv_sem2)
-        all_ref[...] = panel_ref[...]
+        panels(n_row, n_col, local_ref, panel_ref, out_ref, low_ref)
         for side in range(2):
             @pl.when(x_there[side])
             def _():
@@ -586,7 +608,6 @@
     blocks = n_x // ROWS
     f32, bf16 = jnp.float32, jnp.bfloat16
     last = n_z // 2 - 1
-    pieces = jax.ShapeDtypeStruct((n_sub, depth, width), f32)
     return pl.pallas_call(
         functools.partial(main_kernel, n_row, n_col),
         grid=(n_z // 2 + 1,),
@@ -595,8 +616,8 @@
             pl.BlockSpec((vectors, 2, n_x, n_y), lambda p: (0, jnp.minimum(p, last), 0, 0)),
             pl.BlockSpec((2, n_x, n_y), lambda p: (jnp.minimum(p, last), 0, 0)),
         ],
-        out_specs=[pl.BlockSpec((n_sub, depth, width), lambda g: (0, 0, 0))] * 2,
-        out_shape=[pieces, pieces],
+        out_specs=pl.BlockSpec((n_sub, depth, width), lambda p: (0, 0, 0)),
+        out_shape=jax.ShapeDtypeStruct((n_sub, depth, width), f32),
         scratch_shapes=[
             pltpu.VMEM((2 * n_y, 2 * n_y), bf16),
             pltpu.VMEM((vectors * n_x, 2 * n_y), f32),
@@ -627,6 +648,8 @@
             pltpu.VMEM((n_sub, depth, width), f32),
             pltpu.VMEM((depth, width), f32),
             pltpu.VMEM((n_sub, depth, width), f32),
+            pltpu.VMEM((n_sub, depth, width), f32),
+            pltpu.VMEM((2 * PSUB * vectors, 2 * n_col // (2 * PSUB) * width), f32),
             pltpu.SemaphoreType.DMA((2,)),
             pltpu.SemaphoreType.DMA((2,)),
             pltpu.SemaphoreType.DMA((2,)),
@@ -637,7 +660,7 @@
             pltpu.SemaphoreType.DMA((n_sub,)),
         ],
         compiler_params=pltpu.CompilerParams(
-            collective_id=0, has_side_effects=True, vmem_limit_bytes=48 * 1024 * 1024),
+            collective_id=0, has_side_effects=True, vmem_limit_bytes=62200 * 1024),
     )(mobility, own, labels)
 
 
@@ -646,8 +669,7 @@
     n_col = lax.axis_size("col")
     n_sub = n_row * n_col
     vectors = own.shape[0]
-    local, gathered = main_call(own, labels, mobility, n_row, n_col)
-    local = panel_call(local, gathered, n_row, n_col)
+    local = main_call(own, labels, mobility, n_row, n_col)
     return local.reshape(
         n_sub, vectors // (NB * n_col), 1, NB, vectors // (NB * n_row), 1, NB, n_sub
     )

time: 68.7 us -> 62.2 us (0.905)
  Pallas kernels: 65.4 us -> 59.9 us
  local copies, waits for them, and re-layouts: 3.12 us -> 2.14 us
    pallas_call x1 -> x0, Pallas kernels: 11.7 us -> none  [panel_call(): pl.pallas_call(functools.partial(panel_kernel, n_row, n_col), in_specs=[w...]
    pallas_call x1, Pallas kernels: 53.7 us -> 59.9 us  [main_call(): pl.pallas_call(functools.partial(main_kernel, n_row, n_col), grid=(n_z //...]
    unnamed x4 -> x0, local copies, waits for them, and re-layouts: 1.88 us -> none
    reshape x1, local copies, waits for them, and re-layouts: 1.24 us -> 2.14 us  [body(): local.reshape(n_sub, vectors // (NB * n_col), 1, NB, vectors // (NB * n_r...]
where the time goes in v5:
time: 62.2 us; the launch traced here: 62 us
  Pallas kernels  59.9 us (96%)
  local copies, waits for them, and re-layouts  2.14 us (3%)
    pallas_call x1, Pallas kernels, main_call(): pl.pallas_call(functools.partial(main_kernel, n_row, n_col), grid=(n_z //...  59.9 us
    reshape x1, local copies, waits for them, and re-layouts, body(): local.reshape(n_sub, vectors // (NB * n_col), 1, NB, vectors // (NB * n_r...  2.14 us

profile of v5, /device:TPU:0, one launch (start us, length us, event | category | flops | bytes accessed | tf_op | source)
XLA Modules:
  0.0 62.0 jit_solution(18223557721332633648)
XLA Ops:
  0.0 59.9 %shard_map.37 = f32[32,8,128]{2,1,0:T(8,128)} custom-call(f32[4]{0:T(128)} %mob_ref.1, bf16[32,32,64,128]{3,2,1,0:T(8,128)(2,1)} %own_ref.1, s32[32,64,128]{2,1,0:T(8,128)} %lab_ref.1), custom_call_target="tpu_custom_call" | custom-call | tf_op jit(solution)/shard_map/pallas_call | solution.py:611
  59.9 2.1 %reshape.3 = f32[32,4,1,2,2,1,2,32]{7,6,4,3,1,0,5,2:T(2,128)} reshape(f32[32,8,128]{2,1,0:T(8,128)} %shard_map.37) | data formatting | bytes 262144 | tf_op jit(solution)/shard_map/reshape | solution.py:673

commit v6 on v5

--- a/solution.py
+++ b/solution.py
@@ -61,9 +61,10 @@
     c = lax.axis_index("col")
     me = r * n_col + c
 
+    upper = 2 * me // n_sub
+
     def peer(k):
-        other = lax.rem(me + k, n_sub)
-        return other, (other // n_col, lax.rem(other, n_col))
+        return lax.rem(me + upper * k + (1 - upper) * (n_sub - k), n_sub)
 
     at = lax.broadcasted_iota(jnp.int32, (vectors, vectors), 0)
     source = (at // NB % col_blocks * n_col + at // (NB * col_blocks)) * NB + at % NB
@@ -78,78 +79,111 @@
         for row in range(n_row):
             send_ref[row * n_col + column] = tiles[row]
 
-    def exchange(source_of, target_ref, sends, recvs, meanwhile=None):
-        def copy(k):
-            other, where = peer(k)
+    def exchange(source_of, target_ref, sends, recvs):
+        def copy(other):
             return pltpu.make_async_remote_copy(
                 src_ref=source_of(other), dst_ref=target_ref.at[me], send_sem=sends.at[other], recv_sem=recvs.at[me],
-                device_id=where, device_id_type=MESH)
-
-        def begin(k, carry):
-            copy(k).start()
-            return carry
-
-        lax.fori_loop(1, n_sub, begin, 0)
-        if meanwhile:
-            meanwhile()
-
-        def finish(k, carry):
-            other, where = peer(k)
-            pltpu.make_async_remote_copy(
-                src_ref=source_of(other), dst_ref=target_ref.at[other], send_sem=sends.at[other],
-                recv_sem=recvs.at[other], device_id=where, device_id_type=MESH).wait_recv()
-            return carry
-
-        lax.fori_loop(1, n_sub, finish, 0)
-
-        def drain(k, carry):
-            copy(k).wait_send()
-            return carry
-
-        lax.fori_loop(1, n_sub, drain, 0)
-
+                device_id=(other // n_col, lax.rem(other, n_col)), device_id_type=MESH)
+
+        def begin():
+            def one(k, carry):
+                copy(peer(k)).start()
+                return carry
+
+            lax.fori_loop(1, n_sub, one, 0)
+
+        def finish(first, last):
+            def one(other, carry):
+                @pl.when(other != me)
+                def _():
+                    pltpu.make_async_remote_copy(
+                        src_ref=source_of(other), dst_ref=target_ref.at[other], send_sem=sends.at[other],
+                        recv_sem=recvs.at[other], device_id=(other // n_col, lax.rem(other, n_col)),
+                        device_id_type=MESH).wait_recv()
+
+                return carry
+
+            lax.fori_loop(first, last, one, 0)
+
+        def drain():
+            def one(k, carry):
+                copy(peer(k)).wait_send()
+                return carry
+
+            lax.fori_loop(1, n_sub, one, 0)
+
+        return begin, finish, drain
+
+    offsets = slot_offsets()
+    quads = n_sub // n_row
+    lanes = lax.broadcasted_iota(jnp.int32, (depth, width), 1) % n_sub
+    ends, reach = 2 * PSUB, 2 * n_col
+
+    def banded(values):
+        bands = {}
+        for (start, stop), value in zip(offsets, values):
+            shift = start[0] * n_col + start[1]
+            if shift:
+                value = pltpu.roll(value, shift % width, 1)
+            step = (stop[0] - start[0]) * n_col + stop[1] - start[1]
+            bands[step] = bands[step] + value if step in bands else value
+        return bands
+
+    def place(bands, b):
+        value = jnp.zeros((depth, width), jnp.float32)
+        for step, band in bands.items():
+            if 0 <= b - step < n_sub:
+                value = jnp.where(lanes == b - step, band, value)
+        return value
+
+    begin, finish, drain = exchange(lambda other: send_ref.at[other], here_ref, send_sem, recv_sem)
+    begin2, finish2, drain2 = exchange(lambda other: mine_ref, all_ref, send_sem2, recv_sem2)
+    low_bits = [(bit, NB * bit) for bit in powers(n_row)]
     here_ref[me] = send_ref[me]
-    exchange(lambda other: send_ref.at[other], here_ref, send_sem, recv_sem)
-
-    tiles = [here_ref[s] for s in range(n_sub)]
-    quads = n_sub // n_row
-    bits = [(bit, NB * bit) for bit in powers(n_row)]
-    bits += [(n_row * bit, vectors * bit) for bit in powers(quads)]
-    tiles = swap_bits(tiles, bits)
-    offsets = slot_offsets()
+    begin()
+
+    finish(0, n_row)
+    tiles = swap_bits([here_ref[s] for s in range(n_row)], low_bits)
+    packs = -(-SLOTS // quads)
+    stack = jnp.concatenate(tiles[:packs], axis=0)
+    shape = (width, quads * width)
+    lane = lax.broadcasted_iota(jnp.int32, shape, 0)
+    goal = lax.broadcasted_iota(jnp.int32, shape, 1)
+    sub, tru = goal % n_sub, goal % width // n_sub
+    origin = goal // width * vectors + (tru // NB * n_row + sub) * NB + tru % NB
+    stack = exact_dot(stack, ((origin == lane) & (sub < n_row)).astype(jnp.float32))
+    values = []
+    for slot in range(SLOTS):
+        k, quad = divmod(slot, quads)
+        values.append(stack[k * depth : k * depth + depth, quad * width : quad * width + width])
+    bands = banded(values)
+    packed = jnp.zeros((depth, width), jnp.float32)
+    for b in range(ends):
+        value = jnp.where(lanes < reach, place(bands, b), 0.0)
+        packed = packed + (pltpu.roll(value, reach * b, 1) if b else value)
+    mine_ref[...] = packed
+    all_ref[me] = packed
+    begin2()
+
+    finish(n_row, n_sub)
+    bits = low_bits + [(n_row * bit, vectors * bit) for bit in powers(quads)]
+    tiles = swap_bits([here_ref[s] for s in range(n_sub)], bits)
     stack = jnp.concatenate([tiles[slot % quads * n_row + slot // quads] for slot in range(SLOTS)], axis=0)
     into = lax.broadcasted_iota(jnp.int32, (width, width), 1)
     sub, tru = into % n_sub, into // n_sub
     origin = sub // n_row * vectors + (tru // NB * n_row + sub % n_row) * NB + tru % NB
     order = (origin == lax.broadcasted_iota(jnp.int32, (width, width), 0)).astype(jnp.float32)
     stack = exact_dot(stack, order)
-    bands = {}
-    for slot, (start, stop) in enumerate(offsets):
-        value = stack[slot * depth : slot * depth + depth]
-        shift = start[0] * n_col + start[1]
-        if shift:
-            value = pltpu.roll(value, shift % width, 1)
-        step = (stop[0] - start[0]) * n_col + stop[1] - start[1]
-        bands[step] = bands[step] + value if step in bands else value
-    lanes = lax.broadcasted_iota(jnp.int32, (depth, width), 1) % n_sub
-    ends = 2 * PSUB
-    reach = 2 * n_col
-    packed = jnp.zeros((depth, width), jnp.float32)
-
-    def place(b):
-        value = jnp.zeros((depth, width), jnp.float32)
-        for step, band in bands.items():
-            if 0 <= b - step < n_sub:
-                value = jnp.where(lanes == b - step, band, value)
-        out_ref[b] = value
-        return value
-
-    for b in range(ends):
-        value = jnp.where(lanes < reach, place(b), 0.0)
-        packed = packed + (pltpu.roll(value, reach * b, 1) if b else value)
-    mine_ref[...] = packed
-    all_ref[me] = packed
-    exchange(lambda other: mine_ref, all_ref, send_sem2, recv_sem2, lambda: [place(b) for b in range(ends, n_sub)])
+    bands = banded([stack[slot * depth : slot * depth + depth] for slot in range(SLOTS)])
+    for b in range(ends, n_sub):
+        out_ref[b] = place(bands, b)
+    finish2(0, n_sub)
+
+    def settle():
+        drain()
+        drain2()
+
+    return settle
 
 
 def panels(n_row, n_col, local_ref, all_ref, out_ref, low_ref):
@@ -359,17 +393,19 @@
     quarter = n_x // SPOTS
     spot = lax.broadcasted_iota(jnp.int32, (quarter, n_y), 1) % SPOTS
 
-    def one(v, carry):
-        for to, column in enumerate((1, 2)):
-            total = jnp.zeros((quarter, n_y), jnp.float32)
-            for k in range(SPOTS):
-                part = side_ref[v, k * quarter : k * quarter + quarter].astype(jnp.float32)
-                part = pltpu.roll(part, (k - column) % n_y, 1) if k != column else part
-                total = jnp.where(spot == k, part, total)
-            pack_ref[to, v] = total.astype(jnp.bfloat16)
+    def some(m, carry):
+        for v in range(4):
+            v = 4 * m + v
+            for to, column in enumerate((1, 2)):
+                total = jnp.zeros((quarter, n_y), jnp.float32)
+                for k in range(SPOTS):
+                    part = side_ref[v, k * quarter : k * quarter + quarter].astype(jnp.float32)
+                    part = pltpu.roll(part, (k - column) % n_y, 1) if k != column else part
+                    total = jnp.where(spot == k, part, total)
+                pack_ref[to, v] = total.astype(jnp.bfloat16)
         return carry
 
-    lax.fori_loop(0, vectors, one, 0)
+    lax.fori_loop(0, vectors // 4, some, 0)
 
 
 def x_tiles(tiles_ref, frims_ref, xhalo_ref, rootx_ref, faces_ref, ends_ref):
@@ -518,8 +554,12 @@
 
         lax.fori_loop(1, n_sub, greet, 0)
         cross_ref[...] = cross_weights(side_ref.shape[2])
-        for ref in (first_ref, plain0_ref, plain1_ref, part_ref, rows0_ref, rows1_ref, root_ref, acc_ref, side_ref, rooty_ref):
+        for ref in (plain1_ref, part_ref, rows1_ref, root_ref, acc_ref, side_ref, rooty_ref):
             ref[...] = jnp.zeros_like(ref)
+        rim = jnp.zeros((vectors, ROWS, side_ref.shape[2]), jnp.float32)
+        for ref in (first_ref, plain0_ref):
+            ref[:, :ROWS] = rim
+            ref[:, ROWS + side_ref.shape[1] :] = rim
         tiles_ref[:, SLOTS * vectors :] = jnp.zeros((vectors, tiles_ref.shape[1] - SLOTS * vectors), jnp.float32)
         for side in range(2):
             @pl.when(jnp.logical_not(x_there[side]))
@@ -586,9 +626,10 @@
             def _():
                 column_copy(way).wait_recv()
         y_tiles(tiles_ref, acc_ref, side_ref, rooty_ref, yhalo_ref, ends_ref, left_ref, right_ref, cut_ref)
-        trade(n_row, n_col, tiles_ref, local_ref, panel_ref, message_ref, mine_ref, here_ref,
+        settle = trade(n_row, n_col, tiles_ref, local_ref, panel_ref, message_ref, mine_ref, here_ref,
               send_sem, recv_sem, send_sem2, recv_sem2)
         panels(n_row, n_col, local_ref, panel_ref, out_ref, low_ref)
+        settle()
         for side in range(2):
             @pl.when(x_there[side])
             def _():

time: 62.2 us -> 58.5 us (0.941)
  Pallas kernels: 59.9 us -> 56.2 us
    pallas_call x1, Pallas kernels: 59.9 us -> 56.2 us  [main_call(): pl.pallas_call(functools.partial(main_kernel, n_row, n_col), grid=(n_z //...]
where the time goes in v6:
time: 58.5 us; the launch traced here: 58.3 us
  Pallas kernels  56.2 us (96%)
  local copies, waits for them, and re-layouts  2.14 us (4%)
    pallas_call x1, Pallas kernels, main_call(): pl.pallas_call(functools.partial(main_kernel, n_row, n_col), grid=(n_z //...  56.2 us
    reshape x1, local copies, waits for them, and re-layouts, body(): local.reshape(n_sub, vectors // (NB * n_col), 1, NB, vectors // (NB * n_r...  2.14 us

profile of v6, /device:TPU:0, one launch (start us, length us, event | category | flops | bytes accessed | tf_op | source)
XLA Modules:
  0.0 58.3 jit_solution(13077698582535369716)
XLA Ops:
  0.0 56.2 %shard_map.37 = f32[32,8,128]{2,1,0:T(8,128)} custom-call(f32[4]{0:T(128)} %mob_ref.1, bf16[32,32,64,128]{3,2,1,0:T(8,128)(2,1)} %own_ref.1, s32[32,64,128]{2,1,0:T(8,128)} %lab_ref.1), custom_call_target="tpu_custom_call" | custom-call | tf_op jit(solution)/shard_map/pallas_call | solution.py:652
  56.2 2.1 %reshape.3 = f32[32,4,1,2,2,1,2,32]{7,6,4,3,1,0,5,2:T(2,128)} reshape(f32[32,8,128]{2,1,0:T(8,128)} %shard_map.37) | data formatting | bytes 262144 | tf_op jit(solution)/shard_map/reshape | solution.py:714

commit v7 on v6

--- a/solution.py
+++ b/solution.py
@@ -348,6 +348,7 @@
                 for s, value in enumerate((own, next_own)):
                     lines_ref[s, 0, v : v + 1] = value[:1]
                     lines_ref[s, 1, v : v + 1] = value[n_x - 1 :]
+                for s in range(2):
                     turned = pltpu.roll(own_ref[v, s], lax.rem(SPOTS * (z + s) + 2, n_y), 1)
                     side_ref[v] = jnp.where(kept[s], turned, side_ref[v])
                 lines_ref[3, 0, v : v + 1] = flux[:1]
@@ -428,14 +429,16 @@
         tiles_ref[:, at + 2 * vectors : at + 3 * vectors] = gram[vectors:, vectors:]
 
 
-def fold(square, vectors):
-    order = square.shape[0]
+def fold(squares, vectors):
+    order = squares[0].shape[0]
     line = lax.broadcasted_iota(jnp.int32, (order, order), 0)
     column = lax.broadcasted_iota(jnp.int32, (order, order), 1)
+    same = line % ROWS == column % ROWS
     pick = (lax.broadcasted_iota(jnp.int32, (order, vectors), 0) // ROWS
             == lax.broadcasted_iota(jnp.int32, (order, vectors), 1)).astype(jnp.float32)
-    thick = jnp.where(line % ROWS == column % ROWS, square, 0.0).reshape(vectors, ROWS, order).sum(1)
-    return exact_dot(thick, pick)
+    thick = [jnp.where(same, square, 0.0).reshape(vectors, ROWS, order).sum(1) for square in squares]
+    thin = exact_dot(jnp.concatenate(thick, axis=0), pick)
+    return [thin[i * vectors : (i + 1) * vectors] for i in range(len(squares))]
 
 
 def y_tiles(tiles_ref, acc_ref, side_ref, rooty_ref, yhalo_ref, ends_ref, left_ref, right_ref, cut_ref):
@@ -491,17 +494,21 @@
     def put(slot, value):
         tiles_ref[:, slot * vectors : (slot + 1) * vectors] = value
 
-    put(0, fold(acc_ref[...] + edges, vectors))
+    squares = [acc_ref[...] + edges]
+    for side in range(2):
+        here = slice(side * order, side * order + order)
+        squares += [crossed[:order, here], crossed[order:, here]]
+    folded = fold(squares, vectors)
+    put(0, folded[0])
     for side in range(2):
         flux = cut_ref[2 + side].astype(bf16)
         for slot, left, right in ((1 + 3 * side, ends_ref[side], flux), (2 + 3 * side, flux, ends_ref[side])):
             here = slice(slot * vectors, (slot + 1) * vectors)
             tiles_ref[:, here] = tiles_ref[:, here] + lax.dot_general(left, right, MINOR, preferred_element_type=f32)
-        here = slice(side * order, side * order + order)
-        cross = fold(crossed[:order, here], vectors)
+        cross = folded[1 + 2 * side]
         put(7 + 3 * side, cross.T)
         put(8 + 3 * side, cross)
-        put(9 + 3 * side, fold(crossed[order:, here], vectors))
+        put(9 + 3 * side, folded[2 + 2 * side])
     thin = lax.broadcasted_iota(jnp.int32, (vectors, n_y), 1)
     slot = 13
     for x in range(2):
@@ -701,8 +708,8 @@
             pltpu.SemaphoreType.DMA((n_sub,)),
         ],
         compiler_params=pltpu.CompilerParams(
-            collective_id=0, has_side_effects=True, vmem_limit_bytes=62200 * 1024),
-    )(mobility, own, labels)
+            collective_id=0, has_side_effects=True, vmem_limit_bytes=48 * 1024 * 1024),
+    )(pltpu.with_memory_space_constraint(mobility, pltpu.HBM), own, pltpu.with_memory_space_constraint(labels, pltpu.HBM))
 
 
 def body(own, labels, mobility):

time: 58.5 us -> 56.9 us (0.973)
  local copies, waits for them, and re-layouts: 2.14 us -> 1.23 us
  Pallas kernels: 56.2 us -> 55.5 us
    reshape x1, local copies, waits for them, and re-layouts: 2.14 us -> 1.23 us  [body(): local.reshape(n_sub, vectors // (NB * n_col), 1, NB, vectors // (NB * n_r...]
    pallas_call x1, Pallas kernels: 56.2 us -> 55.5 us  [main_call(): pl.pallas_call(functools.partial(main_kernel, n_row, n_col), grid=(n_z //...]
where the time goes in v7:
time: 56.9 us; the launch traced here: 56.8 us
  Pallas kernels  55.5 us (98%)
  local copies, waits for them, and re-layouts  1.23 us (2%)
    pallas_call x1, Pallas kernels, main_call(): pl.pallas_call(functools.partial(main_kernel, n_row, n_col), grid=(n_z //...  55.5 us
    reshape x1, local copies, waits for them, and re-layouts, body(): local.reshape(n_sub, vectors // (NB * n_col), 1, NB, vectors // (NB * n_r...  1.23 us

profile of v7, /device:TPU:0, one launch (start us, length us, event | category | flops | bytes accessed | tf_op | source)
XLA Modules:
  0.0 56.8 jit_solution(3074895571135092605)
XLA Ops:
  0.0 55.5 %shard_map.37 = f32[32,8,128]{2,1,0:T(8,128)S(1)} custom-call(f32[4]{0:T(128)} %mob_ref.1, bf16[32,32,64,128]{3,2,1,0:T(8,128)(2,1)} %own_ref.1, s32[32,64,128]{2,1,0:T(8,128)} %lab_ref.1), custom_call_target="tpu_custom_call" | custom-call | tf_op jit(solution)/shard_map/pallas_call | solution.py:659
  55.5 1.2 %reshape.3 = f32[32,4,1,2,2,1,2,32]{7,6,4,3,1,0,5,2:T(2,128)} reshape(f32[32,8,128]{2,1,0:T(8,128)S(1)} %shard_map.37) | data formatting | bytes 262144 | tf_op jit(solution)/shard_map/reshape | solution.py:721
